TPU v7x, 32 devices: a whole 2x2x4 slice. The times are simulated.
32 devices in a mesh: elem: 8 (over z, core), front: 4 (over y, x).
Axes of the slice: x: 2, y: 2, z: 4, core: 2. Of those that a mesh axis runs over, the one named last changes fastest.
Arguments:
- elem_mat: bfloat16 [24, 24, 4096], P(None, None, ('elem', 'front')), may hold values from -1.25 to 1.25
- elem_deriv: bfloat16 [24, 24, 4096], P(None, None, ('elem', 'front')), may hold values from -1.1953125 to 1.1953125
- elem_disp: bfloat16 [24, 4096], P(None, ('elem', 'front')), may hold values from -6 to 6
- elem_sens: bfloat16 [4096, 24, 512], P(('elem', 'front')), may hold values from -3 to 3
- design_var: int32 [4096], P(('elem', 'front')), may hold values from 0 to 511
- dof_rows: int32 [24, 4096], P(None, ('elem', 'front')), may hold values from 0 to 14336, as said below
- inverse_factor: bfloat16 [57344, 8192], P('front', 'elem'), may hold values from -2 to 2
- coupling: bfloat16 [8192, 49152], P('elem', 'front'), may hold values from -0.0625 to 0.0625
- front_sizes: int32 [7], replicated, may hold values from 4096 to 8192
Outputs:
- sens: float32 [57344, 512], P('front', 'elem')
Inputs may be any that keep to these rules, and one draw needn't show every extreme that they name: `dof_rows`: the used rows of one element lie in one aligned block of 128 rows; the value 14336 marks a degree of freedom that no front holds.
All inputs are finite; a program needn't handle non-finite values.
Results may differ from a plain program's by a relative error of at most 0.014.
Values may be sent and summed in bfloat16 or wider, within the bound.
A program may use at most 128 MiB of HBM per device.

v0:
```python
import jax
import jax.numpy as jnp
from jax import lax
from jax.sharding import PartitionSpec as P

FS = 8192
LEVELS = 3


def swapped(array, axis, bit):
    return lax.ppermute(array, axis, [(i, i ^ 1 << bit) for i in range(lax.axis_size(axis))])


def form_loads(tables, derivs, disps, sens_block, variables, places, column_base, spot_rows):
    column_count = sens_block.shape[2]
    pseudo = -jnp.einsum("ije,ejc->eic", tables, sens_block, preferred_element_type=jnp.float32)
    drive_term = -jnp.einsum("ije,je->ei", derivs, disps, preferred_element_type=jnp.float32)
    column_ids = column_base + lax.iota(jnp.int32, column_count)
    hit_column = (column_ids[None, :] == variables[:, None]).astype(jnp.float32)
    pseudo = pseudo + drive_term[:, :, None] * hit_column[:, None, :]
    term_rows = jnp.zeros((spot_rows, column_count), jnp.float32)
    return term_rows.at[places.T.reshape(-1)].add(pseudo.reshape(-1, column_count), mode="drop")


def gather_group(local_block, bit_count, device):
    if bit_count == 0:
        return local_block
    for bit_at in range(bit_count):
        partner = swapped(local_block, "front", bit_at)
        is_upper = device >> bit_at & 1 == 1
        local_block = jnp.where(
            is_upper,
            jnp.concatenate([partner, local_block], 0),
            jnp.concatenate([local_block, partner], 0),
        )
    return local_block


def reduce_group(partial_value, bit_count, device):
    if bit_count == 0:
        return partial_value
    for bit_at in reversed(range(bit_count)):
        half_rows = partial_value.shape[0] // 2
        lower_half = partial_value[:half_rows]
        upper_half = partial_value[half_rows:]
        is_upper = device >> bit_at & 1 == 1
        kept_half = jnp.where(is_upper, upper_half, lower_half)
        sent_half = jnp.where(is_upper, lower_half, upper_half)
        partial_value = kept_half + swapped(sent_half, "front", bit_at)
    return partial_value


def to_row_block(local_block, bit_count, device):
    whole_front = gather_group(local_block, bit_count, device)
    return lax.all_to_all(whole_front, "elem", split_axis=0, concat_axis=1, tiled=True)


def from_row_block(partial_value, bit_count, device):
    spread = lax.all_to_all(partial_value, "elem", split_axis=1, concat_axis=0, tiled=True)
    return reduce_group(spread, bit_count, device)


def body(
    elem_mat,
    elem_deriv,
    elem_disp,
    elem_sens,
    design_var,
    dof_rows,
    inverse_factor,
    coupling,
    front_sizes,
):
    front_count = lax.axis_size("front")
    depth_bits = front_count.bit_length() - 1
    device = lax.axis_index("front")
    spot_rows = inverse_factor.shape[0]
    own_sens = lax.all_to_all(elem_sens, "elem", split_axis=2, concat_axis=0, tiled=True)
    tables, derivs, disps = (
        lax.all_gather(elem_mat, "elem", axis=2, tiled=True),
        lax.all_gather(elem_deriv, "elem", axis=2, tiled=True),
        lax.all_gather(elem_disp, "elem", axis=1, tiled=True),
    )
    variables, places = (
        lax.all_gather(design_var, "elem", axis=0, tiled=True),
        lax.all_gather(dof_rows, "elem", axis=1, tiled=True),
    )
    column_base = lax.axis_index("elem") * own_sens.shape[2]
    load_rows = form_loads(
        tables, derivs, disps, own_sens, variables, places, column_base, spot_rows
    )
    level_facts = []
    offset = 0
    first_front = 0
    for level_at in range(LEVELS):
        bit_count = depth_bits - (LEVELS - 1 - level_at)
        block_rows = FS >> bit_count
        front_id = first_front + (device >> bit_count)
        size_now = lax.dynamic_index_in_dim(front_sizes, front_id, 0, keepdims=False)
        rows_at = (device & (1 << bit_count) - 1) * block_rows + lax.iota(jnp.int32, block_rows)
        live_rows = (rows_at < size_now).astype(jnp.float32)[:, None]
        level_facts.append((bit_count, block_rows, offset, live_rows))
        offset = offset + block_rows
        first_front = first_front + (1 << LEVELS - 1 - level_at)
    forward_out = []
    acc_rows = None
    for level_at in range(LEVELS):
        bit_count, block_rows, offset, live_rows = level_facts[level_at]
        given = load_rows[offset : offset + block_rows]
        if acc_rows is not None:
            given = given - acc_rows
        rhs_in = (live_rows * given).astype(jnp.bfloat16)
        rhs_rows = to_row_block(rhs_in, bit_count, device)
        factor_rows = inverse_factor[offset : offset + block_rows]
        partial_value = jnp.dot(factor_rows, rhs_rows, preferred_element_type=jnp.float32)
        solved = live_rows * lax.psum_scatter(
            partial_value, "elem", scatter_dimension=1, tiled=True
        )
        forward_out.append(solved)
        if level_at < LEVELS - 1:
            wide_solved = lax.all_gather(solved.astype(jnp.bfloat16), "elem", axis=1, tiled=True)
            links = coupling[:, offset : offset + block_rows]
            parent_part = jnp.dot(links, wide_solved, preferred_element_type=jnp.float32)
            acc_rows = from_row_block(parent_part, bit_count + 1, device)
    pieces_out = [None] * LEVELS
    parent_rows = None
    for level_at in reversed(range(LEVELS)):
        bit_count, block_rows, offset, live_rows = level_facts[level_at]
        residual = forward_out[level_at]
        if parent_rows is not None:
            parent_block = to_row_block(parent_rows, bit_count + 1, device)
            links = coupling[:, offset : offset + block_rows]
            correction = lax.dot_general(
                links, parent_block, (((0,), (0,)), ((), ())), preferred_element_type=jnp.float32
            )
            residual = residual - lax.psum_scatter(
                correction, "elem", scatter_dimension=1, tiled=True
            )
        back_in = (live_rows * residual).astype(jnp.bfloat16)
        wide_back = lax.all_gather(back_in, "elem", axis=1, tiled=True)
        factor_rows = inverse_factor[offset : offset + block_rows]
        partial_value = lax.dot_general(
            factor_rows, wide_back, (((0,), (0,)), ((), ())), preferred_element_type=jnp.float32
        )
        answer = live_rows * from_row_block(partial_value, bit_count, device)
        pieces_out[level_at] = answer
        parent_rows = answer.astype(jnp.bfloat16)
    return jnp.concatenate(pieces_out, 0)


def solution(mesh):
    return jax.shard_map(
        body,
        mesh=mesh,
        in_specs=(
            P(None, None, ("elem", "front")),
            P(None, None, ("elem", "front")),
            P(None, ("elem", "front")),
            P(("elem", "front"), None, None),
            P(("elem", "front")),
            P(None, ("elem", "front")),
            P("front", "elem"),
            P("elem", "front"),
            P(),
        ),
        out_specs=P("front", "elem"),
        check_vma=False,
    )
```

profile of v0, /device:TPU:0, one launch (start us, length us, event | category | flops | bytes accessed | tf_op | source)
XLA Modules:
  0.0 1891.1 jit_solution(9125538343845212889)
XLA Ops:
  19.9 95.3 %all_gather.30 = s32[24,1024]{1,0:T(8,128)S(1)} all-gather(s32[24,128]{1,0:T(8,128)S(1)} %copy-done.3), channel_id=1, replica_groups=mesh['elem'=8,'front'=4] {'elem'}, dimensions={1}, use_global_device_ids=true | all-gather | bytes 110592 | tf_op jit(solution)/shard_map/all_gather | solution.py:86
  171.0 134.3 %scatter_custom_fusion = f32[14336,64]{1,0:T(8,128)} fusion(s32[24576]{0:T(1024)S(1)} %bitcast.156, f32[24576,64]{1,0:T(8,128)} %bitcast.120, f32[]{:T(128)} %constant.14.clone.1), kind=kCustom, calls=%fused_computation.27 | custom fusion | flops 1572864 | bytes 3670528 | tf_op jit(solution)/shard_map/scatter-add | solution.py:22
  312.7 29.2 %all_to_all.184 = bf16[8,1024,64]{1,2,0:T(8,128)(2,1)S(1)} all-to-all(bf16[8,1024,64]{1,2,0:T(8,128)(2,1)S(1)} %bitcast.137), channel_id=1, replica_groups=mesh['elem'=8,'front'=4] {'elem'}, dimensions={0} | all-to-all | bytes 2097152 | tf_op jit(solution)/shard_map/all_to_all | solution.py:55
  357.8 167.2 %reduce-scatter.6.cloned.1.call-done = f32[8192,64]{0,1:T(8,128)} async-done(((f32[8192,512]{0,1:T(8,128)}), f32[8192,64]{0,1:T(8,128)}) %reduce-scatter.6.cloned.1.call-update) | async-done | bytes 2097168 | tf_op jit(solution)/shard_map/reduce_scatter | solution.py:116
  527.7 80.6 %all-gather.13.cloned.1.call-done = bf16[8192,512]{0,1:T(8,128)(2,1)} async-done(((bf16[8192,64]{0,1:T(8,128)(2,1)}), bf16[8192,512]{0,1:T(8,128)(2,1)}) %all-gather.13.cloned.1.call-update) | async-done | bytes 8388624 | tf_op jit(solution)/shard_map/all_gather | solution.py:121
  627.8 48.9 %all-to-all-done.2 = f32[1024,8,64]{0,2,1:T(8,128)S(1)} async-done(((f32[1024,8,64]{0,2,1:T(8,128)}), f32[1024,8,64]{0,2,1:T(8,128)S(1)}, u32[]{:S(2)}, u32[]{:S(2)}) %all-to-all-start.2) | async-done | bytes 2097184 | tf_op jit(solution)/shard_map/all_to_all | solution.py:59
  718.3 29.9 %all_to_all.185 = bf16[8,1024,64]{1,2,0:T(8,128)(2,1)S(1)} all-to-all(bf16[8,1024,64]{1,2,0:T(8,128)(2,1)S(1)} %bitcast.138), channel_id=1, replica_groups=mesh['elem'=8,'front'=4] {'elem'}, dimensions={0} | all-to-all | bytes 2097152 | tf_op jit(solution)/shard_map/all_to_all | solution.py:55
  758.6 88.3 %reduce-scatter.8.cloned.1.call-done = f32[4096,64]{0,1:T(8,128)} async-done(((f32[4096,512]{0,1:T(8,128)}), f32[4096,64]{0,1:T(8,128)}) %reduce-scatter.8.cloned.1.call-update) | async-done | bytes 1048592 | tf_op jit(solution)/shard_map/reduce_scatter | solution.py:116
  849.0 45.5 %all-gather.15.cloned.1.call-done = bf16[4096,512]{0,1:T(8,128)(2,1)} async-done(((bf16[4096,64]{0,1:T(8,128)(2,1)}), bf16[4096,512]{0,1:T(8,128)(2,1)}) %all-gather.15.cloned.1.call-update) | async-done | bytes 4194320 | tf_op jit(solution)/shard_map/all_gather | solution.py:121
  908.7 48.9 %all-to-all-done.4 = f32[1024,8,64]{0,2,1:T(8,128)S(1)} async-done(((f32[1024,8,64]{0,2,1:T(8,128)}), f32[1024,8,64]{0,2,1:T(8,128)S(1)}, u32[]{:S(2)}, u32[]{:S(2)}) %all-to-all-start.4) | async-done | bytes 2097184 | tf_op jit(solution)/shard_map/all_to_all | solution.py:59
  959.6 23.0 %collective-permute-done.2 = f32[4096,64]{0,1:T(8,128)S(1)} collective-permute-done((f32[4096,64]{0,1:T(8,128)S(1)}, f32[4096,64]{0,1:T(8,128)S(1)}, u32[]{:S(2)}, u32[]{:S(2)}) %collective-permute-start.2) | collective-permute-done | bytes 1048608 | tf_op jit(solution)/shard_map/ppermute | solution.py:11
  1014.1 30.9 %all_to_all.186 = bf16[8,1024,64]{1,2,0:T(8,128)(2,1)S(1)} all-to-all(bf16[8,1024,64]{1,2,0:T(8,128)(2,1)S(1)} %bitcast.139), channel_id=1, replica_groups=mesh['elem'=8,'front'=4] {'elem'}, dimensions={0} | all-to-all | bytes 2097152 | tf_op jit(solution)/shard_map/all_to_all | solution.py:55
  1051.6 48.9 %reduce-scatter.10.cloned.1.call-done = f32[2048,64]{0,1:T(8,128)} async-done(((f32[2048,512]{0,1:T(8,128)}), f32[2048,64]{0,1:T(8,128)}) %reduce-scatter.10.cloned.1.call-update) | async-done | bytes 524304 | tf_op jit(solution)/shard_map/reduce_scatter | solution.py:116
  1102.4 27.7 %all-gather.17.cloned.1.call-done = bf16[2048,512]{0,1:T(8,128)(2,1)} async-done(((bf16[2048,64]{0,1:T(8,128)(2,1)}), bf16[2048,512]{0,1:T(8,128)(2,1)}) %all-gather.17.cloned.1.call-update) | async-done | bytes 2097168 | tf_op jit(solution)/shard_map/all_gather | solution.py:140
  1135.3 51.9 %all_to_all.187 = f32[1024,8,64]{0,2,1:T(8,128)S(1)} all-to-all(f32[1024,8,64]{0,2,1:T(8,128)S(1)} %bitcast.144), channel_id=1, replica_groups=mesh['elem'=8,'front'=4] {'elem'}, dimensions={1} | all-to-all | bytes 4194304 | tf_op jit(solution)/shard_map/all_to_all | solution.py:59
  1243.1 31.4 %all_to_all.188 = bf16[8,1024,64]{1,2,0:T(8,128)(2,1)S(1)} all-to-all(bf16[8,1024,64]{1,2,0:T(8,128)(2,1)S(1)} %bitcast.140), channel_id=1, replica_groups=mesh['elem'=8,'front'=4] {'elem'}, dimensions={0} | all-to-all | bytes 2097152 | tf_op jit(solution)/shard_map/all_to_all | solution.py:55
  1284.7 88.5 %reduce-scatter.12.cloned.1.call-done = f32[4096,64]{0,1:T(8,128)} async-done(((f32[4096,512]{0,1:T(8,128)}), f32[4096,64]{0,1:T(8,128)}) %reduce-scatter.12.cloned.1.call-update) | async-done | bytes 1048592 | tf_op jit(solution)/shard_map/reduce_scatter | solution.py:136
  1375.4 45.4 %all-gather.19.cloned.1.call-done = bf16[4096,512]{0,1:T(8,128)(2,1)} async-done(((bf16[4096,64]{0,1:T(8,128)(2,1)}), bf16[4096,512]{0,1:T(8,128)(2,1)}) %all-gather.19.cloned.1.call-update) | async-done | bytes 4194320 | tf_op jit(solution)/shard_map/all_gather | solution.py:140
  1429.0 51.5 %all_to_all.189 = f32[1024,8,64]{0,2,1:T(8,128)S(1)} all-to-all(f32[1024,8,64]{0,2,1:T(8,128)S(1)} %bitcast.145), channel_id=1, replica_groups=mesh['elem'=8,'front'=4] {'elem'}, dimensions={1} | all-to-all | bytes 4194304 | tf_op jit(solution)/shard_map/all_to_all | solution.py:59
  1482.5 23.0 %collective-permute-done.10 = f32[4096,64]{0,1:T(8,128)S(1)} collective-permute-done((f32[4096,64]{0,1:T(8,128)S(1)}, f32[4096,64]{0,1:T(8,128)S(1)}, u32[]{:S(2)}, u32[]{:S(2)}) %collective-permute-start.10) | collective-permute-done | bytes 1048608 | tf_op jit(solution)/shard_map/ppermute | solution.py:11
  1518.5 30.1 %all_to_all.190 = bf16[8,1024,64]{1,2,0:T(8,128)(2,1)S(1)} all-to-all(bf16[8,1024,64]{1,2,0:T(8,128)(2,1)S(1)} %bitcast.141), channel_id=1, replica_groups=mesh['elem'=8,'front'=4] {'elem'}, dimensions={0} | all-to-all | bytes 2097152 | tf_op jit(solution)/shard_map/all_to_all | solution.py:55
  1564.4 167.1 %reduce-scatter.14.cloned.1.call-done = f32[8192,64]{0,1:T(8,128)} async-done(((f32[8192,512]{0,1:T(8,128)}), f32[8192,64]{0,1:T(8,128)}) %reduce-scatter.14.cloned.1.call-update) | async-done | bytes 2097168 | tf_op jit(solution)/shard_map/reduce_scatter | solution.py:136
  1734.3 80.6 %all-gather.21.cloned.1.call-done = bf16[8192,512]{0,1:T(8,128)(2,1)} async-done(((bf16[8192,64]{0,1:T(8,128)(2,1)}), bf16[8192,512]{0,1:T(8,128)(2,1)}) %all-gather.21.cloned.1.call-update) | async-done | bytes 8388624 | tf_op jit(solution)/shard_map/all_gather | solution.py:140
  1829.2 51.5 %all_to_all.191 = f32[1024,8,64]{0,2,1:T(8,128)S(1)} all-to-all(f32[1024,8,64]{0,2,1:T(8,128)S(1)} %bitcast.146), channel_id=1, replica_groups=mesh['elem'=8,'front'=4] {'elem'}, dimensions={1} | all-to-all | bytes 4194304 | tf_op jit(solution)/shard_map/all_to_all | solution.py:59
  (143 shorter events, 357.0 us)
Async XLA Ops:
  6.5 137.2 %all-gather.11.cloned.1.call-start = ((), (), s32[]{:S(2)}) async-start(), calls=%async_computation.17 | async-start | bytes 1327104 | tf_op jit(solution)/shard_map/all_gather | solution.py:81
  12.6 143.2 %all-to-all-start = ((bf16[128,24,512]{0,1,2:T(8,128)(2,1)}), bf16[128,24,512]{0,1,2:T(8,128)(2,1)S(1)}, u32[]{:S(2)}, u32[]{:S(2)}) async-start(bf16[128,24,512]{0,1,2:T(8,128)(2,1)} %copy.36), calls=%async_computation | async-start | bytes 6291456 | tf_op jit(solution)/shard_map/all_to_all | solution.py:78
  19.1 129.2 %all-gather.9.cloned.1.call-start = ((), (), s32[]{:S(2)}) async-start(), calls=%async_computation.16 | async-start | bytes 1327104 | tf_op jit(solution)/shard_map/all_gather | solution.py:80
  19.9 505.1 %reduce-scatter.6.cloned.1.call-start = ((), (), s32[]{:S(2)}) async-start(), calls=%async_computation.18 | async-start | bytes 18874368 | tf_op jit(solution)/shard_map/reduce_scatter | solution.py:116
  357.8 250.6 %all-gather.13.cloned.1.call-start = ((), (), s32[]{:S(2)}) async-start(), calls=%async_computation.19 | async-start | bytes 9437184 | tf_op jit(solution)/shard_map/all_gather | solution.py:121
  624.2 52.6 %all-to-all-start.2 = ((f32[1024,8,64]{0,2,1:T(8,128)}), f32[1024,8,64]{0,2,1:T(8,128)S(1)}, u32[]{:S(2)}, u32[]{:S(2)}) async-start(f32[1024,8,64]{0,2,1:T(8,128)} %bitcast.143), calls=%async_computation.3 | async-start | bytes 4194304 | tf_op jit(solution)/shard_map/all_to_all | solution.py:59
  627.8 219.1 %reduce-scatter.8.cloned.1.call-start = ((), (), s32[]{:S(2)}) async-start(), calls=%async_computation.20 | async-start | bytes 9437184 | tf_op jit(solution)/shard_map/reduce_scatter | solution.py:116
  679.0 24.9 %collective-permute-start = (f32[4096,64]{0,1:T(8,128)}, f32[4096,64]{0,1:T(8,128)}, u32[]{:S(2)}, u32[]{:S(2)}) collective-permute-start(f32[4096,64]{0,1:T(8,128)} %bitcast.67), channel_id=1, source_target_pairs={{0,1},{1,0},{2,3},{3,2},{4,5},{5,4},{6,7},{7,6},{8,9},{9,8},{10,11... | collective-permute-start | bytes 3145736 | tf_op jit(solution)/shard_map/ppermute | solution.py:11
  705.3 12.6 collective-permute-start.1
  758.4 136.1 %all-gather.15.cloned.1.call-start = ((), (), s32[]{:S(2)}) async-start(), calls=%async_computation.21 | async-start | bytes 4718592 | tf_op jit(solution)/shard_map/all_gather | solution.py:121
  905.0 52.6 %all-to-all-start.4 = ((f32[1024,8,64]{0,2,1:T(8,128)}), f32[1024,8,64]{0,2,1:T(8,128)S(1)}, u32[]{:S(2)}, u32[]{:S(2)}) async-start(f32[1024,8,64]{0,2,1:T(8,128)} %bitcast.142), calls=%async_computation.6 | async-start | bytes 4194304 | tf_op jit(solution)/shard_map/all_to_all | solution.py:59
  908.6 191.9 %reduce-scatter.10.cloned.1.call-start = ((), (), s32[]{:S(2)}) async-start(), calls=%async_computation.22 | async-start | bytes 4718592 | tf_op jit(solution)/shard_map/reduce_scatter | solution.py:116
  957.9 24.7 %collective-permute-start.2 = (f32[4096,64]{0,1:T(8,128)S(1)}, f32[4096,64]{0,1:T(8,128)S(1)}, u32[]{:S(2)}, u32[]{:S(2)}) collective-permute-start(f32[4096,64]{0,1:T(8,128)S(1)} %bitcast.147), channel_id=1, source_target_pairs={{0,2},{1,3},{2,0},{3,1},{4,6},{5,7},{6,4},{7,5},{8,10},{9,11},{10,... | collective-permute-start | bytes 3145736 | tf_op jit(solution)/shard_map/ppermute | solution.py:11
  982.8 12.7 collective-permute-start.3
  1003.2 10.6 collective-permute-start.5
  1051.6 78.5 %all-gather.17.cloned.1.call-start = ((), (), s32[]{:S(2)}) async-start(), calls=%async_computation.23 | async-start | bytes 2359296 | tf_op jit(solution)/shard_map/all_gather | solution.py:140
  1102.3 270.9 %reduce-scatter.12.cloned.1.call-start = ((), (), s32[]{:S(2)}) async-start(), calls=%async_computation.24 | async-start | bytes 9437184 | tf_op jit(solution)/shard_map/reduce_scatter | solution.py:136
  1187.6 24.6 %collective-permute-start.6 = (f32[4096,64]{0,1:T(8,128)S(1)}, f32[4096,64]{0,1:T(8,128)S(1)}, u32[]{:S(2)}, u32[]{:S(2)}) collective-permute-start(f32[4096,64]{0,1:T(8,128)S(1)} %bitcast.148), channel_id=1, source_target_pairs={{0,2},{1,3},{2,0},{3,1},{4,6},{5,7},{6,4},{7,5},{8,10},{9,11},{10,... | collective-permute-start | bytes 3145736 | tf_op jit(solution)/shard_map/ppermute | solution.py:11
  1212.4 12.5 collective-permute-start.7
  1284.7 136.2 %all-gather.19.cloned.1.call-start = ((), (), s32[]{:S(2)}) async-start(), calls=%async_computation.25 | async-start | bytes 4718592 | tf_op jit(solution)/shard_map/all_gather | solution.py:140
  1375.4 356.1 %reduce-scatter.14.cloned.1.call-start = ((), (), s32[]{:S(2)}) async-start(), calls=%async_computation.26 | async-start | bytes 18874368 | tf_op jit(solution)/shard_map/reduce_scatter | solution.py:136
  1480.9 24.6 %collective-permute-start.10 = (f32[4096,64]{0,1:T(8,128)S(1)}, f32[4096,64]{0,1:T(8,128)S(1)}, u32[]{:S(2)}, u32[]{:S(2)}) collective-permute-start(f32[4096,64]{0,1:T(8,128)S(1)} %bitcast.149), channel_id=1, source_target_pairs={{0,1},{1,0},{2,3},{3,2},{4,5},{5,4},{6,7},{7,6},{8,9},{9,8},{10,11... | collective-permute-start | bytes 3145736 | tf_op jit(solution)/shard_map/ppermute | solution.py:11
  1505.6 12.5 collective-permute-start.11
  1564.3 250.6 %all-gather.21.cloned.1.call-start = ((), (), s32[]{:S(2)}) async-start(), calls=%async_computation.27 | async-start | bytes 9437184 | tf_op jit(solution)/shard_map/all_gather | solution.py:140
  (12 other events, 643.7 us)
Sparse Core Ops, SparseCore 0:
  8.9 42.0 all-gather.10
  52.6 45.5 all-gather.8
  357.9 167.0 reduce-scatter.5
  527.8 80.4 all-gather.12
  758.5 88.3 reduce-scatter.7
  849.1 45.3 all-gather.14
  1051.7 48.7 reduce-scatter.9
  1102.4 27.6 all-gather.16
  1284.8 88.3 reduce-scatter.11
  1375.5 45.3 all-gather.18
  1564.4 167.0 reduce-scatter.13
  1734.4 80.4 all-gather.20
where the time goes:
time: 1900 us; the launch traced here: 1890 us
  waiting for transfers between devices  1100 us (58%)
  blocking collectives  426 us (22%)
  other arithmetic  162 us (9%)
  matrix products  122 us (6%)
  local copies, waits for them, and re-layouts  35 us (2%)
  starting transfers between devices  32.6 us (2%)
    reduce_scatter x3, waiting for transfers between devices, body(): lax.psum_scatter(partial_value, 'elem', scatter_dimension=1, tiled=True)  304 us
    reduce_scatter x2, waiting for transfers between devices, body(): lax.psum_scatter(correction, 'elem', scatter_dimension=1, tiled=True)  256 us
    ppermute x12, waiting for transfers between devices, swapped(): lax.ppermute(array, axis, [(i, i ^ 1 << bit) for i in range(lax.axis_size...  161 us
    all_to_all x3, blocking collectives, from_row_block(): lax.all_to_all(partial_value, 'elem', split_axis=1, concat_axis=0, tiled=...  155 us
    all_gather x3, waiting for transfers between devices, body(): wide_back = lax.all_gather(back_in, 'elem', axis=1, tiled=True)  154 us
    all_to_all x5, blocking collectives, to_row_block(): lax.all_to_all(whole_front, 'elem', split_axis=0, concat_axis=1, tiled=True)  152 us
    scatter-add x1, other arithmetic, form_loads(): term_rows.at[places.T.reshape(-1)]  134 us
    all_gather x2, waiting for transfers between devices, body(): lax.all_gather(solved.astype(jnp.bfloat16), 'elem', axis=1, tiled=True)  126 us
  transfers between devices with their start and end apart: 27, of which 24 were waited for; matrix products, arithmetic and copies ran while one was open for 1% of the time, Pallas kernels for 0%

commit v1 on v0

v1 whole, which is shorter than its diff:
```python
import jax
import jax.numpy as jnp
from jax import lax
from jax.sharding import PartitionSpec as P

FS = 8192
LEVELS = 3
CHUNKS = 2


def swapped(array, axis, bit):
    return lax.ppermute(array, axis, [(i, i ^ 1 << bit) for i in range(lax.axis_size(axis))])


def local_pseudo(tables, derivs, disps, sens, variables):
    column_count = sens.shape[2]
    pseudo = -jnp.einsum("ije,ejc->eic", tables, sens, preferred_element_type=jnp.float32)
    drive_term = -jnp.einsum("ije,je->ei", derivs, disps, preferred_element_type=jnp.float32)
    column_ids = lax.iota(jnp.int32, column_count)
    hit_column = (column_ids[None, :] == variables[:, None]).astype(jnp.float32)
    return pseudo + drive_term[:, :, None] * hit_column[:, None, :]


def scatter_rows(pseudo, places, spot_rows):
    column_count = pseudo.shape[-1]
    term_rows = jnp.zeros((spot_rows, column_count), jnp.float32)
    return term_rows.at[places.T.reshape(-1)].add(
        pseudo.reshape(-1, column_count).astype(jnp.float32), mode="drop"
    )


def sum_group(value, bits):
    for bit_at in bits:
        value = value + swapped(value.astype(jnp.bfloat16), "front", bit_at).astype(jnp.float32)
    return value


def body(
    elem_mat,
    elem_deriv,
    elem_disp,
    elem_sens,
    design_var,
    dof_rows,
    inverse_factor,
    coupling,
    front_sizes,
):
    bf16, f32 = jnp.bfloat16, jnp.float32
    depth_bits = lax.axis_size("front").bit_length() - 1
    elem_count = lax.axis_size("elem")
    device = lax.axis_index("front")
    elem_at = lax.axis_index("elem")
    inner = FS // elem_count
    spot_rows = inverse_factor.shape[0]

    pseudo = local_pseudo(elem_mat, elem_deriv, elem_disp, elem_sens, design_var).astype(bf16)
    places = lax.all_gather(dof_rows, "elem", axis=1, tiled=True)
    own_pseudo = lax.all_to_all(pseudo, "elem", split_axis=2, concat_axis=0, tiled=True)
    load_rows = scatter_rows(own_pseudo, places, spot_rows).astype(bf16)

    facts = []
    offset = 0
    first_front = 0
    for level_at in range(LEVELS):
        bit_count = depth_bits - (LEVELS - 1 - level_at)
        block_rows = FS >> bit_count
        front_id = first_front + (device >> bit_count)
        size_now = lax.dynamic_index_in_dim(front_sizes, front_id, 0, keepdims=False)
        start = (device & (1 << bit_count) - 1) * block_rows
        shard = block_rows // elem_count
        own_at = start + elem_at * shard + lax.iota(jnp.int32, shard)
        inner_at = elem_at * inner + lax.iota(jnp.int32, inner)
        own_live = (own_at < size_now).astype(f32)[:, None]
        inner_live = (inner_at < size_now).astype(f32)[:, None]
        facts.append((bit_count, block_rows, offset, start, own_live, inner_live))
        offset = offset + block_rows
        first_front = first_front + (1 << LEVELS - 1 - level_at)

    given = []
    for level_at in range(LEVELS):
        bit_count, block_rows, offset, start, own_live, inner_live = facts[level_at]
        piece = load_rows[offset : offset + block_rows]
        if block_rows < FS:
            spread = jnp.zeros((FS, piece.shape[1]), bf16)
            piece = lax.dynamic_update_slice_in_dim(spread, piece, start, 0)
        given.append(lax.all_to_all(piece, "elem", split_axis=0, concat_axis=1, tiled=True))

    width = given[0].shape[1] // CHUNKS

    def bits_of(bit_count, chunk):
        bits = list(range(bit_count))
        return bits if chunk % 2 == 0 else bits[::-1]

    def scatter_sum(partial_value):
        return lax.psum_scatter(
            partial_value.astype(bf16), "elem", scatter_dimension=0, tiled=True
        ).astype(f32)

    def widen(value):
        return lax.all_gather(value.astype(bf16), "elem", axis=0, tiled=True)

    forward_out = [[None] * CHUNKS for _ in range(LEVELS)]
    wide_out = [None] * CHUNKS
    part = [given[0][:, c * width : (c + 1) * width].astype(f32) for c in range(CHUNKS)]
    for level_at in range(LEVELS):
        bit_count, block_rows, offset, start, own_live, inner_live = facts[level_at]
        factor_rows = inverse_factor[offset : offset + block_rows]
        for c in range(CHUNKS):
            rhs = (inner_live * sum_group(part[c], bits_of(bit_count, c))).astype(bf16)
            solved = own_live * scatter_sum(jnp.dot(factor_rows, rhs, preferred_element_type=f32))
            forward_out[level_at][c] = solved
            wide_out[c] = widen(solved)
            if level_at < LEVELS - 1:
                links = coupling[:, offset : offset + block_rows]
                acc = jnp.dot(links, wide_out[c], preferred_element_type=f32)
                part[c] = given[level_at + 1][:, c * width : (c + 1) * width].astype(f32) - acc

    pieces_out = [None] * LEVELS
    parent = [None] * CHUNKS
    for level_at in reversed(range(LEVELS)):
        bit_count, block_rows, offset, start, own_live, inner_live = facts[level_at]
        factor_rows = inverse_factor[offset : offset + block_rows]
        links = coupling[:, offset : offset + block_rows] if level_at < LEVELS - 1 else None
        for c in range(CHUNKS):
            if level_at == LEVELS - 1:
                wide_back = wide_out[c]
            else:
                correction = lax.dot_general(
                    links, parent[c], (((0,), (0,)), ((), ())), preferred_element_type=f32
                )
                residual = forward_out[level_at][c] - scatter_sum(correction)
                wide_back = widen(own_live * residual)
            partial_value = lax.dot_general(
                factor_rows, wide_back, (((0,), (0,)), ((), ())), preferred_element_type=f32
            )
            answer = inner_live * sum_group(partial_value, bits_of(bit_count, c))
            parent[c] = answer.astype(bf16)
        whole = jnp.concatenate(parent, 1)
        turned = lax.all_to_all(whole, "elem", split_axis=1, concat_axis=0, tiled=True)
        pieces_out[level_at] = lax.dynamic_slice_in_dim(turned, start, block_rows, 0)
    return jnp.concatenate(pieces_out, 0).astype(f32)


def solution(mesh):
    return jax.shard_map(
        body,
        mesh=mesh,
        in_specs=(
            P(None, None, ("elem", "front")),
            P(None, None, ("elem", "front")),
            P(None, ("elem", "front")),
            P(("elem", "front"), None, None),
            P(("elem", "front")),
            P(None, ("elem", "front")),
            P("front", "elem"),
            P("elem", "front"),
            P(),
        ),
        out_specs=P("front", "elem"),
        check_vma=False,
    )
```

time: 1900 us -> 1450 us (0.76)
  waiting for transfers between devices: 1100 us -> 842 us
  blocking collectives: 426 us -> 178 us
  matrix products: 122 us -> 167 us
    all_to_all x8 -> x2, blocking collectives: 306 us -> 100 us  [body(): lax.all_to_all(piece, 'elem', split_axis=0, concat_axis=1, tiled=True)]
    reduce_scatter x5 -> x10, waiting for transfers between devices: 560 us -> 368 us  [scatter_sum(): lax.psum_scatter(partial_value.astype(bf16), 'elem', scatter_dimension=0,...]
    all_gather x7 -> x10, waiting for transfers between devices: 280 us -> 223 us  [widen(): return lax.all_gather(value.astype(bf16), 'elem', axis=0, tiled=True)]
    all_gather x3 -> x1, blocking collectives: 119 us -> 77.8 us  [body(): places = lax.all_gather(dof_rows, 'elem', axis=1, tiled=True)]
    dot_general x8 -> x15, matrix products: 94 us -> 124 us  [the longest x6 42.9 us: body(): jnp.dot(factor_rows, rhs, preferred_element_type=f32)]
    dot_general x3 -> x6, matrix products: 27.6 us -> 43.3 us  [body(): lax.dot_general(factor_rows, wide_back, (((0,), (0,)), ((), ())), preferr...]
    all_to_all x3 -> x5, waiting for transfers between devices: 97.8 us -> 100 us  [the longest x3 75 us: body(): lax.all_to_all(whole, 'elem', split_axis=1, concat_axis=0, tiled=True)]
  transfers between devices with their start and end apart: 27 -> 37, of which waited for: 24 -> 35; matrix products, arithmetic and copies ran while one was open for 1% -> 5% of each run, Pallas kernels for 0% -> 0%
where the time goes in v1:
time: 1450 us; the launch traced here: 1440 us
  waiting for transfers between devices  842 us (58%)
  blocking collectives  178 us (12%)
  other arithmetic  171 us (12%)
  matrix products  167 us (12%)
  starting transfers between devices  39.5 us (3%)
  local copies, waits for them, and re-layouts  30.6 us (2%)
  between operations  14.6 us (1%)
    reduce_scatter x10, waiting for transfers between devices, scatter_sum(): lax.psum_scatter(partial_value.astype(bf16), 'elem', scatter_dimension=0,...  368 us
    all_gather x10, waiting for transfers between devices, widen(): return lax.all_gather(value.astype(bf16), 'elem', axis=0, tiled=True)  223 us
    ppermute x12, waiting for transfers between devices, swapped(): lax.ppermute(array, axis, [(i, i ^ 1 << bit) for i in range(lax.axis_size...  149 us
    scatter-add x1, other arithmetic, scatter_rows(): term_rows.at[places.T.reshape(-1)]  134 us
    all_to_all x2, blocking collectives, body(): lax.all_to_all(piece, 'elem', split_axis=0, concat_axis=1, tiled=True)  100 us
    all_gather x1, blocking collectives, body(): places = lax.all_gather(dof_rows, 'elem', axis=1, tiled=True)  77.8 us
    all_to_all x3, waiting for transfers between devices, body(): lax.all_to_all(whole, 'elem', split_axis=1, concat_axis=0, tiled=True)  75 us
    dot_general x6, matrix products, body(): lax.dot_general(factor_rows, wide_back, (((0,), (0,)), ((), ())), preferr...  43.3 us
  transfers between devices with their start and end apart: 37, of which 35 were waited for; matrix products, arithmetic and copies ran while one was open for 5% of the time, Pallas kernels for 0%

profile of v1, /device:TPU:0, one launch (start us, length us, event | category | flops | bytes accessed | tf_op | source)
XLA Modules:
  0.0 1443.4 jit_solution(890690150845639164)
XLA Ops:
  27.3 77.8 %all_gather.33 = s32[24,1024]{1,0:T(8,128)S(1)} all-gather(s32[24,128]{1,0:T(8,128)S(1)} %copy-done.12), channel_id=1, replica_groups=mesh['elem'=8,'front'=4] {'elem'}, dimensions={1}, use_global_device_ids=true | all-gather | bytes 110592 | tf_op jit(solution)/shard_map/all_gather | solution.py:58
  121.2 134.3 %scatter_custom_fusion = f32[14336,64]{1,0:T(8,128)} fusion(s32[24576]{0:T(1024)S(1)} %bitcast.126, f32[24576,64]{1,0:T(8,128)} %bitcast.108, f32[]{:T(128)} %constant.17.clone.1), kind=kCustom, calls=%fused_computation.51 | custom fusion | flops 1572864 | bytes 3670528 | tf_op jit(solution)/shard_map/scatter-add | solution.py:27
  267.7 25.2 %all-to-all-done.1 = bf16[8,1024,64]{1,2,0:T(8,128)(2,1)S(1)} async-done(((bf16[8,1024,64]{1,2,0:T(8,128)(2,1)}), bf16[8,1024,64]{1,2,0:T(8,128)(2,1)S(1)}, u32[]{:S(2)}, u32[]{:S(2)}) %all-to-all-start.1) | async-done | bytes 1048608 | tf_op jit(solution)/shard_map/all_to_all | solution.py:87
  302.4 49.0 %reduce-scatter.11.cloned.1.call-done = bf16[1024,256]{0,1:T(8,128)(2,1)} async-done(((bf16[8192,256]{0,1:T(8,128)(2,1)}), bf16[1024,256]{0,1:T(8,128)(2,1)}) %reduce-scatter.11.cloned.1.call-update) | async-done | bytes 524304 | tf_op jit(solution)/shard_map/reduce_scatter | solution.py:96
  354.2 54.4 %all_to_all.123 = bf16[8,1024,64]{1,2,0:T(8,128)(2,1)S(1)} all-to-all(bf16[8,1024,64]{1,2,0:T(8,128)(2,1)S(1)} %bitcast.114), channel_id=1, replica_groups=mesh['elem'=8,'front'=4] {'elem'}, dimensions={0} | all-to-all | bytes 2097152 | tf_op jit(solution)/shard_map/all_to_all | solution.py:87
  453.3 34.4 %reduce-scatter.13.cloned.1.call-done = bf16[512,256]{0,1:T(8,128)(2,1)} async-done(((bf16[4096,256]{0,1:T(8,128)(2,1)}), bf16[512,256]{0,1:T(8,128)(2,1)}) %reduce-scatter.13.cloned.1.call-update) | async-done | bytes 262160 | tf_op jit(solution)/shard_map/reduce_scatter | solution.py:96
  489.9 46.1 %all_to_all.124 = bf16[8,1024,64]{1,2,0:T(8,128)(2,1)S(1)} all-to-all(bf16[8,1024,64]{1,2,0:T(8,128)(2,1)S(1)} %bitcast.115), channel_id=1, replica_groups=mesh['elem'=8,'front'=4] {'elem'}, dimensions={0} | all-to-all | bytes 2097152 | tf_op jit(solution)/shard_map/all_to_all | solution.py:87
  575.5 30.4 %reduce-scatter.15.cloned.1.call-done = bf16[256,256]{0,1:T(8,128)(2,1)} async-done(((bf16[2048,256]{0,1:T(8,128)(2,1)}), bf16[256,256]{0,1:T(8,128)(2,1)}) %reduce-scatter.15.cloned.1.call-update) | async-done | bytes 131088 | tf_op jit(solution)/shard_map/reduce_scatter | solution.py:96
  607.6 22.1 %all-gather.15.cloned.1.call-done = bf16[2048,256]{0,1:T(8,128)(2,1)} async-done(((bf16[256,256]{0,1:T(8,128)(2,1)}), bf16[2048,256]{0,1:T(8,128)(2,1)}) %all-gather.15.cloned.1.call-update) | async-done | bytes 1048592 | tf_op jit(solution)/shard_map/all_gather | solution.py:101
  668.5 34.9 %reduce-scatter.17.cloned.1.call-done = bf16[512,256]{0,1:T(8,128)(2,1)} async-done(((bf16[4096,256]{0,1:T(8,128)(2,1)}), bf16[512,256]{0,1:T(8,128)(2,1)}) %reduce-scatter.17.cloned.1.call-update) | async-done | bytes 262160 | tf_op jit(solution)/shard_map/reduce_scatter | solution.py:96
  715.3 17.6 %all-gather.17.cloned.1.call-done = bf16[4096,256]{0,1:T(8,128)(2,1)} async-done(((bf16[512,256]{0,1:T(8,128)(2,1)}), bf16[4096,256]{0,1:T(8,128)(2,1)}) %all-gather.17.cloned.1.call-update) | async-done | bytes 2097168 | tf_op jit(solution)/shard_map/all_gather | solution.py:101
  766.2 18.4 %reduce-scatter.21.cloned.1.call-done = bf16[1024,256]{0,1:T(8,128)(2,1)} async-done(((bf16[8192,256]{0,1:T(8,128)(2,1)}), bf16[1024,256]{0,1:T(8,128)(2,1)}) %reduce-scatter.21.cloned.1.call-update) | async-done | bytes 524304 | tf_op jit(solution)/shard_map/reduce_scatter | solution.py:96
  784.6 50.6 %reduce-scatter.19.cloned.1.call-done = bf16[1024,256]{0,1:T(8,128)(2,1)} async-done(((bf16[8192,256]{0,1:T(8,128)(2,1)}), bf16[1024,256]{0,1:T(8,128)(2,1)}) %reduce-scatter.19.cloned.1.call-update) | async-done | bytes 524304 | tf_op jit(solution)/shard_map/reduce_scatter | solution.py:96
  837.9 45.3 %all-gather.21.cloned.1.call-done = bf16[8192,256]{0,1:T(8,128)(2,1)} async-done(((bf16[1024,256]{0,1:T(8,128)(2,1)}), bf16[8192,256]{0,1:T(8,128)(2,1)}) %all-gather.21.cloned.1.call-update) | async-done | bytes 4194320 | tf_op jit(solution)/shard_map/all_gather | solution.py:101
  917.3 35.0 %reduce-scatter.23.cloned.1.call-done = bf16[512,256]{0,1:T(8,128)(2,1)} async-done(((bf16[4096,256]{0,1:T(8,128)(2,1)}), bf16[512,256]{0,1:T(8,128)(2,1)}) %reduce-scatter.23.cloned.1.call-update) | async-done | bytes 262160 | tf_op jit(solution)/shard_map/reduce_scatter | solution.py:96
  954.1 27.9 %all-gather.23.cloned.1.call-done = bf16[4096,256]{0,1:T(8,128)(2,1)} async-done(((bf16[512,256]{0,1:T(8,128)(2,1)}), bf16[4096,256]{0,1:T(8,128)(2,1)}) %all-gather.23.cloned.1.call-update) | async-done | bytes 2097168 | tf_op jit(solution)/shard_map/all_gather | solution.py:101
  1020.4 32.1 %reduce-scatter.25.cloned.1.call-done = bf16[256,256]{0,1:T(8,128)(2,1)} async-done(((bf16[2048,256]{0,1:T(8,128)(2,1)}), bf16[256,256]{0,1:T(8,128)(2,1)}) %reduce-scatter.25.cloned.1.call-update) | async-done | bytes 131088 | tf_op jit(solution)/shard_map/reduce_scatter | solution.py:96
  1054.3 22.0 %all-gather.25.cloned.1.call-done = bf16[2048,256]{0,1:T(8,128)(2,1)} async-done(((bf16[256,256]{0,1:T(8,128)(2,1)}), bf16[2048,256]{0,1:T(8,128)(2,1)}) %all-gather.25.cloned.1.call-update) | async-done | bytes 1048592 | tf_op jit(solution)/shard_map/all_gather | solution.py:101
  1115.0 34.9 %reduce-scatter.27.cloned.1.call-done = bf16[512,256]{0,1:T(8,128)(2,1)} async-done(((bf16[4096,256]{0,1:T(8,128)(2,1)}), bf16[512,256]{0,1:T(8,128)(2,1)}) %reduce-scatter.27.cloned.1.call-update) | async-done | bytes 262160 | tf_op jit(solution)/shard_map/reduce_scatter | solution.py:96
  1151.7 27.7 %all-gather.27.cloned.1.call-done = bf16[4096,256]{0,1:T(8,128)(2,1)} async-done(((bf16[512,256]{0,1:T(8,128)(2,1)}), bf16[4096,256]{0,1:T(8,128)(2,1)}) %all-gather.27.cloned.1.call-update) | async-done | bytes 2097168 | tf_op jit(solution)/shard_map/all_gather | solution.py:101
  1213.3 48.7 %reduce-scatter.29.cloned.1.call-done = bf16[1024,256]{0,1:T(8,128)(2,1)} async-done(((bf16[8192,256]{0,1:T(8,128)(2,1)}), bf16[1024,256]{0,1:T(8,128)(2,1)}) %reduce-scatter.29.cloned.1.call-update) | async-done | bytes 524304 | tf_op jit(solution)/shard_map/reduce_scatter | solution.py:96
  1269.7 52.1 %all-to-all-done.6 = bf16[1024,8,64]{0,2,1:T(8,128)(2,1)S(1)} async-done(((bf16[1024,8,64]{0,2,1:T(8,128)(2,1)}), bf16[1024,8,64]{0,2,1:T(8,128)(2,1)S(1)}, u32[]{:S(2)}, u32[]{:S(2)}) %all-to-all-start.6) | async-done | bytes 1048608 | tf_op jit(solution)/shard_map/all_to_all | solution.py:140
  1342.1 46.1 %all-gather.29.cloned.1.call-done = bf16[8192,256]{0,1:T(8,128)(2,1)} async-done(((bf16[1024,256]{0,1:T(8,128)(2,1)}), bf16[8192,256]{0,1:T(8,128)(2,1)}) %all-gather.29.cloned.1.call-update) | async-done | bytes 4194320 | tf_op jit(solution)/shard_map/all_gather | solution.py:101
  1408.8 22.9 %all-to-all-done.4 = bf16[1024,8,64]{0,2,1:T(8,128)(2,1)} async-done(((bf16[1024,8,64]{0,2,1:T(8,128)(2,1)}), bf16[1024,8,64]{0,2,1:T(8,128)(2,1)}, u32[]{:S(2)}, u32[]{:S(2)}) %all-to-all-start.4) | async-done | bytes 1048608 | tf_op jit(solution)/shard_map/all_to_all | solution.py:140
  (183 shorter events, 439.2 us)
Async XLA Ops:
  20.9 86.7 %all-to-all-start = ((bf16[128,24,512]{0,1,2:T(8,128)(2,1)}), bf16[128,24,512]{0,1,2:T(8,128)(2,1)S(1)}, u32[]{:S(2)}, u32[]{:S(2)}) async-start(bf16[128,24,512]{0,1,2:T(8,128)(2,1)} %copy.53), calls=%async_computation | async-start | bytes 6291456 | tf_op jit(solution)/shard_map/all_to_all | solution.py:59
  266.3 85.1 %reduce-scatter.11.cloned.1.call-start = ((), (), s32[]{:S(2)}) async-start(), calls=%async_computation.17 | async-start | bytes 4718592 | tf_op jit(solution)/shard_map/reduce_scatter | solution.py:96
  302.4 116.1 %all-gather.11.cloned.1.call-start = ((), (), s32[]{:S(2)}) async-start(), calls=%async_computation.18 | async-start | bytes 4718592 | tf_op jit(solution)/shard_map/all_gather | solution.py:101
  353.4 134.3 %reduce-scatter.13.cloned.1.call-start = ((), (), s32[]{:S(2)}) async-start(), calls=%async_computation.19 | async-start | bytes 2359296 | tf_op jit(solution)/shard_map/reduce_scatter | solution.py:96
  452.6 83.9 %all-gather.13.cloned.1.call-start = ((), (), s32[]{:S(2)}) async-start(), calls=%async_computation.20 | async-start | bytes 2359296 | tf_op jit(solution)/shard_map/all_gather | solution.py:101
  489.4 116.5 %reduce-scatter.15.cloned.1.call-start = ((), (), s32[]{:S(2)}) async-start(), calls=%async_computation.21 | async-start | bytes 1179648 | tf_op jit(solution)/shard_map/reduce_scatter | solution.py:96
  574.9 54.9 %all-gather.15.cloned.1.call-start = ((), (), s32[]{:S(2)}) async-start(), calls=%async_computation.22 | async-start | bytes 1179648 | tf_op jit(solution)/shard_map/all_gather | solution.py:101
  607.6 95.8 %reduce-scatter.17.cloned.1.call-start = ((), (), s32[]{:S(2)}) async-start(), calls=%async_computation.23 | async-start | bytes 2359296 | tf_op jit(solution)/shard_map/reduce_scatter | solution.py:96
  668.4 64.5 %all-gather.17.cloned.1.call-start = ((), (), s32[]{:S(2)}) async-start(), calls=%async_computation.24 | async-start | bytes 2359296 | tf_op jit(solution)/shard_map/all_gather | solution.py:101
  705.2 79.4 %reduce-scatter.21.cloned.1.call-start = ((), (), s32[]{:S(2)}) async-start(), calls=%async_computation.27 | async-start | bytes 4718592 | tf_op jit(solution)/shard_map/reduce_scatter | solution.py:96
  714.8 120.3 %reduce-scatter.19.cloned.1.call-start = ((), (), s32[]{:S(2)}) async-start(), calls=%async_computation.25 | async-start | bytes 4718592 | tf_op jit(solution)/shard_map/reduce_scatter | solution.py:96
  766.1 117.0 %all-gather.21.cloned.1.call-start = ((), (), s32[]{:S(2)}) async-start(), calls=%async_computation.28 | async-start | bytes 4718592 | tf_op jit(solution)/shard_map/all_gather | solution.py:101
  837.7 114.6 %reduce-scatter.23.cloned.1.call-start = ((), (), s32[]{:S(2)}) async-start(), calls=%async_computation.29 | async-start | bytes 2359296 | tf_op jit(solution)/shard_map/reduce_scatter | solution.py:96
  917.3 64.6 %all-gather.23.cloned.1.call-start = ((), (), s32[]{:S(2)}) async-start(), calls=%async_computation.30 | async-start | bytes 2359296 | tf_op jit(solution)/shard_map/all_gather | solution.py:101
  954.0 98.5 %reduce-scatter.25.cloned.1.call-start = ((), (), s32[]{:S(2)}) async-start(), calls=%async_computation.31 | async-start | bytes 1179648 | tf_op jit(solution)/shard_map/reduce_scatter | solution.py:96
  1020.3 56.0 %all-gather.25.cloned.1.call-start = ((), (), s32[]{:S(2)}) async-start(), calls=%async_computation.32 | async-start | bytes 1179648 | tf_op jit(solution)/shard_map/all_gather | solution.py:101
  1054.1 95.8 %reduce-scatter.27.cloned.1.call-start = ((), (), s32[]{:S(2)}) async-start(), calls=%async_computation.33 | async-start | bytes 2359296 | tf_op jit(solution)/shard_map/reduce_scatter | solution.py:96
  1115.0 64.5 %all-gather.27.cloned.1.call-start = ((), (), s32[]{:S(2)}) async-start(), calls=%async_computation.34 | async-start | bytes 2359296 | tf_op jit(solution)/shard_map/all_gather | solution.py:101
  1151.7 110.3 %reduce-scatter.29.cloned.1.call-start = ((), (), s32[]{:S(2)}) async-start(), calls=%async_computation.35 | async-start | bytes 4718592 | tf_op jit(solution)/shard_map/reduce_scatter | solution.py:96
  1212.5 118.0 %all-gather.19.cloned.1.call-start = ((), (), s32[]{:S(2)}) async-start(), calls=%async_computation.26 | async-start | bytes 4718592 | tf_op jit(solution)/shard_map/all_gather | solution.py:101
  1213.2 175.0 %all-gather.29.cloned.1.call-start = ((), (), s32[]{:S(2)}) async-start(), calls=%async_computation.36 | async-start | bytes 4718592 | tf_op jit(solution)/shard_map/all_gather | solution.py:101
  1265.1 56.7 %all-to-all-start.6 = ((bf16[1024,8,64]{0,2,1:T(8,128)(2,1)}), bf16[1024,8,64]{0,2,1:T(8,128)(2,1)S(1)}, u32[]{:S(2)}, u32[]{:S(2)}) async-start(bf16[1024,8,64]{0,2,1:T(8,128)(2,1)} %bitcast.44), calls=%async_computation.16 | async-start | bytes 2097152 | tf_op jit(solution)/shard_map/all_to_all | solution.py:140
  1321.8 79.1 %all-to-all-start.5 = ((bf16[1024,8,64]{0,2,1:T(8,128)(2,1)}), bf16[1024,8,64]{0,2,1:T(8,128)(2,1)}, u32[]{:S(2)}, u32[]{:S(2)}) async-start(bf16[1024,8,64]{0,2,1:T(8,128)(2,1)} %bitcast.42), calls=%async_computation.15 | async-start | bytes 2097152 | tf_op jit(solution)/shard_map/all_to_all | solution.py:140
  1400.9 30.8 %all-to-all-start.4 = ((bf16[1024,8,64]{0,2,1:T(8,128)(2,1)}), bf16[1024,8,64]{0,2,1:T(8,128)(2,1)}, u32[]{:S(2)}, u32[]{:S(2)}) async-start(bf16[1024,8,64]{0,2,1:T(8,128)(2,1)} %bitcast.40), calls=%async_computation.14 | async-start | bytes 2097152 | tf_op jit(solution)/shard_map/all_to_all | solution.py:140
  (29 other events, 813.6 us)
Sparse Core Ops, SparseCore 0:
  302.5 48.8 reduce-scatter.10
  353.5 64.9 all-gather.10
  452.7 34.9 reduce-scatter.12
  489.5 46.8 all-gather.12
  575.0 30.9 reduce-scatter.14
  607.7 22.0 all-gather.14
  668.5 34.8 reduce-scatter.16
  705.3 27.5 all-gather.16
  735.2 49.3 reduce-scatter.20
  786.7 48.3 reduce-scatter.18
  837.8 45.3 all-gather.20
  917.4 34.8 reduce-scatter.22
  954.1 27.7 all-gather.22
  1020.4 31.9 reduce-scatter.24
  1054.2 22.0 all-gather.24
  1115.1 34.7 reduce-scatter.26
  1151.8 27.5 all-gather.26
  1212.6 49.3 reduce-scatter.28
  1263.6 66.8 all-gather.18
  1331.9 56.2 all-gather.28

commit v2 on v1

--- a/solution.py
+++ b/solution.py
@@ -1,11 +1,15 @@
 import jax
 import jax.numpy as jnp
 from jax import lax
+from jax.experimental import pallas as pl
+from jax.experimental.pallas import tpu as pltpu
 from jax.sharding import PartitionSpec as P
 
 FS = 8192
 LEVELS = 3
 CHUNKS = 2
+BLK = 128
+GROUP = 8
 
 
 def swapped(array, axis, bit):
@@ -21,12 +25,52 @@
     return pseudo + drive_term[:, :, None] * hit_column[:, None, :]
 
 
+def scatter_kernel(blocks_ref, rows_ref, pseudo_ref, out_ref):
+    out_ref[...] = jnp.zeros_like(out_ref)
+    dof = rows_ref.shape[1]
+
+    def step(group_at, carry):
+        first = pl.multiple_of(group_at * GROUP, GROUP)
+        rows = rows_ref[pl.ds(first, GROUP), :]
+        spread = []
+        for at in range(GROUP):
+            lanes = jnp.broadcast_to(rows[at : at + 1, :], (BLK, dof))
+            hits = lax.broadcasted_iota(jnp.int32, (BLK, dof), 0) == lanes
+            spread.append(
+                jnp.dot(
+                    hits.astype(jnp.float32).astype(jnp.bfloat16),
+                    pseudo_ref[first + at],
+                    preferred_element_type=jnp.float32,
+                )
+            )
+        for at in range(GROUP):
+            block = blocks_ref[first + at]
+            out_ref[block] = out_ref[block] + spread[at]
+        return carry
+
+    lax.fori_loop(0, rows_ref.shape[0] // GROUP, step, 0)
+
+
 def scatter_rows(pseudo, places, spot_rows):
-    column_count = pseudo.shape[-1]
-    term_rows = jnp.zeros((spot_rows, column_count), jnp.float32)
-    return term_rows.at[places.T.reshape(-1)].add(
-        pseudo.reshape(-1, column_count).astype(jnp.float32), mode="drop"
-    )
+    element_count, dof, column_count = pseudo.shape
+    block_count = spot_rows // BLK
+    places = places.T
+    used = places < spot_rows
+    blocks = jnp.min(jnp.where(used, places, spot_rows), 1) // BLK
+    blocks = jnp.clip(blocks, 0, block_count - 1)
+    rows = jnp.where(used, places - blocks[:, None] * BLK, -1)
+    spread = pl.pallas_call(
+        scatter_kernel,
+        out_shape=jax.ShapeDtypeStruct((block_count, BLK, column_count), jnp.float32),
+        in_specs=[
+            pl.BlockSpec(memory_space=pltpu.SMEM),
+            pl.BlockSpec(memory_space=pltpu.VMEM),
+            pl.BlockSpec(memory_space=pltpu.VMEM),
+        ],
+        out_specs=pl.BlockSpec(memory_space=pltpu.VMEM),
+        compiler_params=pltpu.CompilerParams(vmem_limit_bytes=40 * 1024 * 1024),
+    )(blocks, rows, pseudo)
+    return spread.reshape(spot_rows, column_count)
 
 
 def sum_group(value, bits):
@@ -93,52 +137,77 @@
         return bits if chunk % 2 == 0 else bits[::-1]
 
     def scatter_sum(partial_value):
-        return lax.psum_scatter(
-            partial_value.astype(bf16), "elem", scatter_dimension=0, tiled=True
-        ).astype(f32)
+        return lax.psum_scatter(partial_value, "elem", scatter_dimension=0, tiled=True)
 
     def widen(value):
-        return lax.all_gather(value.astype(bf16), "elem", axis=0, tiled=True)
-
-    forward_out = [[None] * CHUNKS for _ in range(LEVELS)]
-    wide_out = [None] * CHUNKS
-    part = [given[0][:, c * width : (c + 1) * width].astype(f32) for c in range(CHUNKS)]
+        return lax.all_gather(value, "elem", axis=0, tiled=True)
+
+    last = []
+
+    def in_turn(chunk, operand, transfer, results):
+        if last:
+            held, at = last.pop()
+            held[at], operand = lax.optimization_barrier((held[at], operand))
+        results[chunk] = transfer(operand)
+        last.append((results, chunk))
+
+    chunks = range(CHUNKS)
+    forward_out = []
+    part = [given[0][:, c * width : (c + 1) * width].astype(f32) for c in chunks]
     for level_at in range(LEVELS):
         bit_count, block_rows, offset, start, own_live, inner_live = facts[level_at]
         factor_rows = inverse_factor[offset : offset + block_rows]
-        for c in range(CHUNKS):
+        sums, wide = [None] * CHUNKS, [None] * CHUNKS
+        for c in chunks:
+            if level_at:
+                links = coupling[:, links_at : links_at + links_rows]
+                acc = jnp.dot(links, wide_before[c], preferred_element_type=f32)
+                part[c] = given[level_at][:, c * width : (c + 1) * width].astype(f32) - acc
             rhs = (inner_live * sum_group(part[c], bits_of(bit_count, c))).astype(bf16)
-            solved = own_live * scatter_sum(jnp.dot(factor_rows, rhs, preferred_element_type=f32))
-            forward_out[level_at][c] = solved
-            wide_out[c] = widen(solved)
-            if level_at < LEVELS - 1:
-                links = coupling[:, offset : offset + block_rows]
-                acc = jnp.dot(links, wide_out[c], preferred_element_type=f32)
-                part[c] = given[level_at + 1][:, c * width : (c + 1) * width].astype(f32) - acc
+            product = jnp.dot(factor_rows, rhs, preferred_element_type=f32).astype(bf16)
+            in_turn(c, product, scatter_sum, sums)
+        for c in chunks:
+            in_turn(c, (own_live * sums[c].astype(f32)).astype(bf16), widen, wide)
+        forward_out.append([own_live * sums[c].astype(f32) for c in chunks])
+        wide_before, links_at, links_rows = wide, offset, block_rows
 
     pieces_out = [None] * LEVELS
-    parent = [None] * CHUNKS
+    answers = [None] * CHUNKS
     for level_at in reversed(range(LEVELS)):
         bit_count, block_rows, offset, start, own_live, inner_live = facts[level_at]
         factor_rows = inverse_factor[offset : offset + block_rows]
-        links = coupling[:, offset : offset + block_rows] if level_at < LEVELS - 1 else None
-        for c in range(CHUNKS):
-            if level_at == LEVELS - 1:
-                wide_back = wide_out[c]
-            else:
+        if level_at == LEVELS - 1:
+            wide = wide_before
+        else:
+            links = coupling[:, offset : offset + block_rows]
+            sums, next_wide = [None] * CHUNKS, [None] * CHUNKS
+            for c in chunks:
+                answers[c] = answer_of(c, upper, wide)
                 correction = lax.dot_general(
-                    links, parent[c], (((0,), (0,)), ((), ())), preferred_element_type=f32
-                )
-                residual = forward_out[level_at][c] - scatter_sum(correction)
-                wide_back = widen(own_live * residual)
+                    links, answers[c], (((0,), (0,)), ((), ())), preferred_element_type=f32
+                ).astype(bf16)
+                in_turn(c, correction, scatter_sum, sums)
+            pieces_out[level_at + 1] = piece_of(answers, upper)
+            for c in chunks:
+                residual = forward_out[level_at][c] - sums[c].astype(f32)
+                in_turn(c, (own_live * residual).astype(bf16), widen, next_wide)
+            wide = next_wide
+
+        def answer_of(chunk, facts_at, wide_rows):
+            rows, live, bits = facts_at[:3]
             partial_value = lax.dot_general(
-                factor_rows, wide_back, (((0,), (0,)), ((), ())), preferred_element_type=f32
+                rows, wide_rows[chunk], (((0,), (0,)), ((), ())), preferred_element_type=f32
             )
-            answer = inner_live * sum_group(partial_value, bits_of(bit_count, c))
-            parent[c] = answer.astype(bf16)
-        whole = jnp.concatenate(parent, 1)
-        turned = lax.all_to_all(whole, "elem", split_axis=1, concat_axis=0, tiled=True)
-        pieces_out[level_at] = lax.dynamic_slice_in_dim(turned, start, block_rows, 0)
+            return (live * sum_group(partial_value, bits_of(bits, chunk))).astype(bf16)
+
+        def piece_of(parts, facts_at):
+            whole = jnp.concatenate(parts, 1)
+            turned = lax.all_to_all(whole, "elem", split_axis=1, concat_axis=0, tiled=True)
+            return lax.dynamic_slice_in_dim(turned, facts_at[3], facts_at[4], 0)
+
+        upper = (factor_rows, inner_live, bit_count, start, block_rows)
+    answers = [answer_of(c, upper, wide) for c in chunks]
+    pieces_out[0] = piece_of(answers, upper)
     return jnp.concatenate(pieces_out, 0).astype(f32)
 
 

time: 1450 us -> 1140 us (0.79)
  waiting for transfers between devices: 842 us -> 681 us
  other arithmetic: 171 us -> 30.7 us
  blocking collectives: 178 us -> 133 us
  Pallas kernels: 0 us -> 29.5 us
    scatter-add x1 -> x0, other arithmetic: 134 us -> none  [scatter_rows(): term_rows.at[places.T.reshape(-1)]]
    reduce_scatter x10, waiting for transfers between devices: 368 us -> 257 us  [scatter_sum(): lax.psum_scatter(partial_value, 'elem', scatter_dimension=0, tiled=True)]
    all_to_all x2 -> x1, blocking collectives: 100 us -> 53.1 us  [body(): lax.all_to_all(piece, 'elem', split_axis=0, concat_axis=1, tiled=True)]
    all_gather x10, waiting for transfers between devices: 223 us -> 182 us  [widen(): return lax.all_gather(value, 'elem', axis=0, tiled=True)]
    pallas_call x0 -> x1, Pallas kernels: none -> 29.5 us  [scatter_rows(): pl.pallas_call(scatter_kernel, out_shape=jax.ShapeDtypeStruct((block_coun...]
  transfers between devices with their start and end apart: 37 -> 38, of which waited for: 35 -> 29; matrix products, arithmetic and copies ran while one was open for 5% -> 16% of each run, Pallas kernels for 0% -> 0%
where the time goes in v2:
time: 1140 us; the launch traced here: 1130 us
  waiting for transfers between devices  681 us (60%)
  matrix products  165 us (14%)
  blocking collectives  133 us (12%)
  starting transfers between devices  42.4 us (4%)
  other arithmetic  30.7 us (3%)
  local copies, waits for them, and re-layouts  29.9 us (3%)
  Pallas kernels  29.5 us (3%)
  between operations  14.7 us (1%)
    reduce_scatter x10, waiting for transfers between devices, scatter_sum(): lax.psum_scatter(partial_value, 'elem', scatter_dimension=0, tiled=True)  257 us
    all_gather x10, waiting for transfers between devices, widen(): return lax.all_gather(value, 'elem', axis=0, tiled=True)  182 us
    ppermute x12, waiting for transfers between devices, swapped(): lax.ppermute(array, axis, [(i, i ^ 1 << bit) for i in range(lax.axis_size...  139 us
    all_gather x1, blocking collectives, body(): places = lax.all_gather(dof_rows, 'elem', axis=1, tiled=True)  79.5 us
    all_to_all x3, waiting for transfers between devices, piece_of(): lax.all_to_all(whole, 'elem', split_axis=1, concat_axis=0, tiled=True)  78.1 us
    all_to_all x1, blocking collectives, body(): lax.all_to_all(piece, 'elem', split_axis=0, concat_axis=1, tiled=True)  53.1 us
    dot_general x6, matrix products, answer_of(): lax.dot_general(rows, wide_rows[chunk], (((0,), (0,)), ((), ())), preferr...  43.4 us
    dot_general x6, matrix products, body(): product = jnp.dot(factor_rows, rhs, preferred_element_type=f32).astype(bf16)  42.9 us
  transfers between devices with their start and end apart: 38, of which 29 were waited for; matrix products, arithmetic and copies ran while one was open for 16% of the time, Pallas kernels for 0%

profile of v2, /device:TPU:0, one launch (start us, length us, event | category | flops | bytes accessed | tf_op | source)
XLA Modules:
  0.0 1125.5 jit_solution(17038781796629791456)
XLA Ops:
  27.5 79.5 %all_gather.33 = s32[24,1024]{0,1:T(8,128)S(1)} all-gather(s32[24,128]{0,1:T(8,128)S(1)} %copy.42), channel_id=1, replica_groups=mesh['elem'=8,'front'=4] {'elem'}, dimensions={1}, use_global_device_ids=true | all-gather | bytes 110592 | tf_op jit(solution)/shard_map/all_gather | solution.py:102
  118.0 29.5 %shard_map.91 = f32[112,128,64]{2,1,0:T(8,128)S(1)} custom-call(s32[1024]{0:T(1024)S(1)} %get-tuple-element.82.blocks_ref, s32[1024,24]{1,0:T(8,128)S(1)} %compare_select_fusion.rows_ref, bf16[1024,24,64]{2,1,0:T(8,128)(2,1)S(1)} %bitcast.113), custom_call_target="tpu_custom_call" | custom-call | tf_op jit(solution)/shard_map/pallas_call | solution.py:62
  157.6 25.1 %all-to-all-done.1 = bf16[8,1024,64]{1,2,0:T(8,128)(2,1)S(1)} async-done(((bf16[8,1024,64]{1,2,0:T(8,128)(2,1)}), bf16[8,1024,64]{1,2,0:T(8,128)(2,1)S(1)}, u32[]{:S(2)}, u32[]{:S(2)}) %all-to-all-start.1) | async-done | bytes 1048608 | tf_op jit(solution)/shard_map/all_to_all | solution.py:131
  202.2 39.1 %reduce-scatter.11.cloned.1.call-done = bf16[1024,256]{0,1:T(8,128)(2,1)} async-done(((bf16[8192,256]{0,1:T(8,128)(2,1)}), bf16[1024,256]{0,1:T(8,128)(2,1)}) %reduce-scatter.11.cloned.1.call-update) | async-done | bytes 524304 | tf_op jit(solution)/shard_map/reduce_scatter | solution.py:140
  243.2 48.8 %reduce-scatter.13.cloned.1.call-done = bf16[1024,256]{0,1:T(8,128)(2,1)} async-done(((bf16[8192,256]{0,1:T(8,128)(2,1)}), bf16[1024,256]{0,1:T(8,128)(2,1)}) %reduce-scatter.13.cloned.1.call-update) | async-done | bytes 524304 | tf_op jit(solution)/shard_map/reduce_scatter | solution.py:140
  294.0 45.0 %all-gather.11.cloned.1.call-done = bf16[8192,256]{0,1:T(8,128)(2,1)} async-done(((bf16[1024,256]{0,1:T(8,128)(2,1)}), bf16[8192,256]{0,1:T(8,128)(2,1)}) %all-gather.11.cloned.1.call-update) | async-done | bytes 4194320 | tf_op jit(solution)/shard_map/all_gather | solution.py:143
  339.6 53.1 %all_to_all.132 = bf16[8,1024,64]{1,2,0:T(8,128)(2,1)S(1)} all-to-all(bf16[8,1024,64]{1,2,0:T(8,128)(2,1)S(1)} %bitcast.121), channel_id=1, replica_groups=mesh['elem'=8,'front'=4] {'elem'}, dimensions={0} | all-to-all | bytes 2097152 | tf_op jit(solution)/shard_map/all_to_all | solution.py:131
  392.7 12.7 %fusion.183 = (bf16[1024,256]{0,1:T(8,128)(2,1)S(1)}, f32[1024,256]{0,1:T(8,128)}) fusion(bf16[8192,256]{0,1:T(8,128)(2,1)} %all-gather.11.cloned.1.call-done, bf16[1024,12288]{1,0:T(8,128)(2,1)} %param.16, bf16[1024,512]{0,1:T(8,128)(2,1)S(1)} %bitcast.129), kind=kOutput, calls=%fused_computation.157 | convolution fusion | flops 4295753728 | bytes 23068672 | tf_op jit(solution)/shard_map/dot_general | solution.py:164
  464.9 33.8 %reduce-scatter.17.cloned.1.call-done = bf16[512,256]{0,1:T(8,128)(2,1)} async-done(((bf16[4096,256]{0,1:T(8,128)(2,1)}), bf16[512,256]{0,1:T(8,128)(2,1)}) %reduce-scatter.17.cloned.1.call-update) | async-done | bytes 262160 | tf_op jit(solution)/shard_map/reduce_scatter | solution.py:140
  504.5 42.6 %all-gather.15.cloned.1.call-done = bf16[4096,256]{0,1:T(8,128)(2,1)} async-done(((bf16[512,256]{0,1:T(8,128)(2,1)}), bf16[4096,256]{0,1:T(8,128)(2,1)}) %all-gather.15.cloned.1.call-update) | async-done | bytes 2097168 | tf_op jit(solution)/shard_map/all_gather | solution.py:143
  555.1 12.6 %collective-permute-done.2 = bf16[1024,256]{0,1:T(8,128)(2,1)S(1)} collective-permute-done((bf16[1024,256]{0,1:T(8,128)(2,1)S(1)}, bf16[1024,256]{0,1:T(8,128)(2,1)S(1)}, u32[]{:S(2)}, u32[]{:S(2)}) %collective-permute-start.2) | collective-permute-done | bytes 524320 | tf_op jit(solution)/shard_map/ppermute | solution.py:16
  623.4 28.5 %reduce-scatter.21.cloned.1.call-done = bf16[256,256]{0,1:T(8,128)(2,1)} async-done(((bf16[2048,256]{0,1:T(8,128)(2,1)}), bf16[256,256]{0,1:T(8,128)(2,1)}) %reduce-scatter.21.cloned.1.call-update) | async-done | bytes 131088 | tf_op jit(solution)/shard_map/reduce_scatter | solution.py:140
  653.6 22.0 %all-gather.19.cloned.1.call-done = bf16[2048,256]{0,1:T(8,128)(2,1)} async-done(((bf16[256,256]{0,1:T(8,128)(2,1)}), bf16[2048,256]{0,1:T(8,128)(2,1)}) %all-gather.19.cloned.1.call-update) | async-done | bytes 1048592 | tf_op jit(solution)/shard_map/all_gather | solution.py:143
  680.4 13.1 %collective-permute-done.6 = bf16[1024,256]{0,1:T(8,128)(2,1)S(1)} collective-permute-done((bf16[1024,256]{0,1:T(8,128)(2,1)S(1)}, bf16[1024,256]{0,1:T(8,128)(2,1)S(1)}, u32[]{:S(2)}, u32[]{:S(2)}) %collective-permute-start.6) | collective-permute-done | bytes 524320 | tf_op jit(solution)/shard_map/ppermute | solution.py:16
  694.4 12.6 %collective-permute-done.7 = bf16[1024,256]{0,1:T(8,128)(2,1)S(1)} collective-permute-done((bf16[1024,256]{0,1:T(8,128)(2,1)S(1)}, bf16[1024,256]{0,1:T(8,128)(2,1)S(1)}, u32[]{:S(2)}, u32[]{:S(2)}) %collective-permute-start.7) | collective-permute-done | bytes 524320 | tf_op jit(solution)/shard_map/ppermute | solution.py:16
  751.9 34.6 %reduce-scatter.25.cloned.1.call-done = bf16[512,256]{0,1:T(8,128)(2,1)} async-done(((bf16[4096,256]{0,1:T(8,128)(2,1)}), bf16[512,256]{0,1:T(8,128)(2,1)}) %reduce-scatter.25.cloned.1.call-update) | async-done | bytes 262160 | tf_op jit(solution)/shard_map/reduce_scatter | solution.py:140
  788.3 27.1 %all-gather.23.cloned.1.call-done = bf16[4096,256]{0,1:T(8,128)(2,1)} async-done(((bf16[512,256]{0,1:T(8,128)(2,1)}), bf16[4096,256]{0,1:T(8,128)(2,1)}) %all-gather.23.cloned.1.call-update) | async-done | bytes 2097168 | tf_op jit(solution)/shard_map/all_gather | solution.py:143
  823.3 12.6 %collective-permute-done.10 = bf16[1024,256]{0,1:T(8,128)(2,1)S(1)} collective-permute-done((bf16[1024,256]{0,1:T(8,128)(2,1)S(1)}, bf16[1024,256]{0,1:T(8,128)(2,1)S(1)}, u32[]{:S(2)}, u32[]{:S(2)}) %collective-permute-start.10) | collective-permute-done | bytes 524320 | tf_op jit(solution)/shard_map/ppermute | solution.py:16
  869.4 12.5 %fusion.28 = bf16[8192,256]{0,1:T(8,128)(2,1)} fusion(bf16[1024,256]{0,1:T(8,128)(2,1)S(1)} %multiply_convert_fusion.2, bf16[1024,12288]{1,0:T(8,128)(2,1)} %param.16), kind=kOutput, calls=%fused_computation.20 | convolution fusion | flops 4297064448 | bytes 21495808 | tf_op jit(solution)/shard_map/dot_general | solution.py:186
  882.0 16.0 %reduce-scatter.27.cloned.1.call-done = bf16[1024,256]{0,1:T(8,128)(2,1)} async-done(((bf16[8192,256]{0,1:T(8,128)(2,1)}), bf16[1024,256]{0,1:T(8,128)(2,1)}) %reduce-scatter.27.cloned.1.call-update) | async-done | bytes 524304 | tf_op jit(solution)/shard_map/reduce_scatter | solution.py:140
  900.0 48.6 %reduce-scatter.29.cloned.1.call-done = bf16[1024,256]{0,1:T(8,128)(2,1)} async-done(((bf16[8192,256]{0,1:T(8,128)(2,1)}), bf16[1024,256]{0,1:T(8,128)(2,1)}) %reduce-scatter.29.cloned.1.call-update) | async-done | bytes 524304 | tf_op jit(solution)/shard_map/reduce_scatter | solution.py:140
  950.7 44.8 %all-gather.27.cloned.1.call-done = bf16[8192,256]{0,1:T(8,128)(2,1)} async-done(((bf16[1024,256]{0,1:T(8,128)(2,1)}), bf16[8192,256]{0,1:T(8,128)(2,1)}) %all-gather.27.cloned.1.call-update) | async-done | bytes 4194320 | tf_op jit(solution)/shard_map/all_gather | solution.py:143
  1002.3 49.9 %all-to-all-done.6 = bf16[1024,8,64]{0,2,1:T(8,128)(2,1)S(1)} async-done(((bf16[1024,8,64]{0,2,1:T(8,128)(2,1)}), bf16[1024,8,64]{0,2,1:T(8,128)(2,1)S(1)}, u32[]{:S(2)}, u32[]{:S(2)}) %all-to-all-start.6) | async-done | bytes 1048608 | tf_op jit(solution)/shard_map/all_to_all | solution.py:205
  1088.3 25.5 %all-to-all-done.4 = bf16[1024,8,64]{0,2,1:T(8,128)(2,1)} async-done(((bf16[1024,8,64]{0,2,1:T(8,128)(2,1)}), bf16[1024,8,64]{0,2,1:T(8,128)(2,1)}, u32[]{:S(2)}, u32[]{:S(2)}) %all-to-all-start.4) | async-done | bytes 1048608 | tf_op jit(solution)/shard_map/all_to_all | solution.py:205
  (180 shorter events, 341.2 us)
Async XLA Ops:
  20.9 86.5 %all-to-all-start = ((bf16[128,24,512]{0,1,2:T(8,128)(2,1)}), bf16[128,24,512]{0,1,2:T(8,128)(2,1)}, u32[]{:S(2)}, u32[]{:S(2)}) async-start(bf16[128,24,512]{0,1,2:T(8,128)(2,1)} %copy.44), calls=%async_computation | async-start | bytes 6291456 | tf_op jit(solution)/shard_map/all_to_all | solution.py:103
  156.1 85.1 %reduce-scatter.11.cloned.1.call-start = ((), (), s32[]{:S(2)}) async-start(), calls=%async_computation.17 | async-start | bytes 4718592 | tf_op jit(solution)/shard_map/reduce_scatter | solution.py:140
  192.2 99.7 %reduce-scatter.13.cloned.1.call-start = ((), (), s32[]{:S(2)}) async-start(), calls=%async_computation.18 | async-start | bytes 4718592 | tf_op jit(solution)/shard_map/reduce_scatter | solution.py:140
  241.3 97.7 %all-gather.11.cloned.1.call-start = ((), (), s32[]{:S(2)}) async-start(), calls=%async_computation.19 | async-start | bytes 4718592 | tf_op jit(solution)/shard_map/all_gather | solution.py:143
  292.0 133.5 %all-gather.13.cloned.1.call-start = ((), (), s32[]{:S(2)}) async-start(), calls=%async_computation.20 | async-start | bytes 4718592 | tf_op jit(solution)/shard_map/all_gather | solution.py:143
  339.0 123.0 %reduce-scatter.15.cloned.1.call-start = ((), (), s32[]{:S(2)}) async-start(), calls=%async_computation.21 | async-start | bytes 2359296 | tf_op jit(solution)/shard_map/reduce_scatter | solution.py:140
  425.5 73.2 %reduce-scatter.17.cloned.1.call-start = ((), (), s32[]{:S(2)}) async-start(), calls=%async_computation.22 | async-start | bytes 2359296 | tf_op jit(solution)/shard_map/reduce_scatter | solution.py:140
  462.0 85.1 %all-gather.15.cloned.1.call-start = ((), (), s32[]{:S(2)}) async-start(), calls=%async_computation.23 | async-start | bytes 2359296 | tf_op jit(solution)/shard_map/all_gather | solution.py:143
  500.1 47.1 %all-to-all-start.3 = ((bf16[8,1024,64]{1,2,0:T(8,128)(2,1)}), bf16[8,1024,64]{1,2,0:T(8,128)(2,1)S(1)}, u32[]{:S(2)}, u32[]{:S(2)}) async-start(bf16[8,1024,64]{1,2,0:T(8,128)(2,1)} %bitcast.111), calls=%async_computation.7 | async-start | bytes 2097152 | tf_op jit(solution)/shard_map/all_to_all | solution.py:131
  503.7 82.1 %all-gather.17.cloned.1.call-start = ((), (), s32[]{:S(2)}) async-start(), calls=%async_computation.24 | async-start | bytes 2359296 | tf_op jit(solution)/shard_map/all_gather | solution.py:143
  547.2 73.9 %reduce-scatter.19.cloned.1.call-start = ((), (), s32[]{:S(2)}) async-start(), calls=%async_computation.25 | async-start | bytes 1179648 | tf_op jit(solution)/shard_map/reduce_scatter | solution.py:140
  585.8 66.1 %reduce-scatter.21.cloned.1.call-start = ((), (), s32[]{:S(2)}) async-start(), calls=%async_computation.26 | async-start | bytes 1179648 | tf_op jit(solution)/shard_map/reduce_scatter | solution.py:140
  621.1 54.5 %all-gather.19.cloned.1.call-start = ((), (), s32[]{:S(2)}) async-start(), calls=%async_computation.27 | async-start | bytes 1179648 | tf_op jit(solution)/shard_map/all_gather | solution.py:143
  651.9 62.4 %all-gather.21.cloned.1.call-start = ((), (), s32[]{:S(2)}) async-start(), calls=%async_computation.28 | async-start | bytes 1179648 | tf_op jit(solution)/shard_map/all_gather | solution.py:143
  680.2 69.8 %reduce-scatter.23.cloned.1.call-start = ((), (), s32[]{:S(2)}) async-start(), calls=%async_computation.29 | async-start | bytes 2359296 | tf_op jit(solution)/shard_map/reduce_scatter | solution.py:140
  714.4 72.1 %reduce-scatter.25.cloned.1.call-start = ((), (), s32[]{:S(2)}) async-start(), calls=%async_computation.30 | async-start | bytes 2359296 | tf_op jit(solution)/shard_map/reduce_scatter | solution.py:140
  750.0 65.4 %all-gather.23.cloned.1.call-start = ((), (), s32[]{:S(2)}) async-start(), calls=%async_computation.31 | async-start | bytes 2359296 | tf_op jit(solution)/shard_map/all_gather | solution.py:143
  786.5 62.0 %all-gather.25.cloned.1.call-start = ((), (), s32[]{:S(2)}) async-start(), calls=%async_computation.32 | async-start | bytes 2359296 | tf_op jit(solution)/shard_map/all_gather | solution.py:143
  815.4 82.6 %reduce-scatter.27.cloned.1.call-start = ((), (), s32[]{:S(2)}) async-start(), calls=%async_computation.33 | async-start | bytes 4718592 | tf_op jit(solution)/shard_map/reduce_scatter | solution.py:140
  848.5 100.1 %reduce-scatter.29.cloned.1.call-start = ((), (), s32[]{:S(2)}) async-start(), calls=%async_computation.34 | async-start | bytes 4718592 | tf_op jit(solution)/shard_map/reduce_scatter | solution.py:140
  898.0 97.5 %all-gather.27.cloned.1.call-start = ((), (), s32[]{:S(2)}) async-start(), calls=%async_computation.35 | async-start | bytes 4718592 | tf_op jit(solution)/shard_map/all_gather | solution.py:143
  948.6 119.1 %all-gather.29.cloned.1.call-start = ((), (), s32[]{:S(2)}) async-start(), calls=%async_computation.36 | async-start | bytes 4718592 | tf_op jit(solution)/shard_map/all_gather | solution.py:143
  996.6 55.5 %all-to-all-start.6 = ((bf16[1024,8,64]{0,2,1:T(8,128)(2,1)}), bf16[1024,8,64]{0,2,1:T(8,128)(2,1)S(1)}, u32[]{:S(2)}, u32[]{:S(2)}) async-start(bf16[1024,8,64]{0,2,1:T(8,128)(2,1)} %bitcast.46), calls=%async_computation.16 | async-start | bytes 2097152 | tf_op jit(solution)/shard_map/all_to_all | solution.py:205
  1052.2 30.8 %all-to-all-start.5 = ((bf16[1024,8,64]{0,2,1:T(8,128)(2,1)}), bf16[1024,8,64]{0,2,1:T(8,128)(2,1)S(1)}, u32[]{:S(2)}, u32[]{:S(2)}) async-start(bf16[1024,8,64]{0,2,1:T(8,128)(2,1)} %bitcast.44), calls=%async_computation.15 | async-start | bytes 2097152 | tf_op jit(solution)/shard_map/all_to_all | solution.py:205
  (28 other events, 533.1 us)
Sparse Core Ops, SparseCore 0:
  192.4 48.8 reduce-scatter.10
  243.5 48.3 reduce-scatter.12
  293.6 45.3 all-gather.10
  340.4 63.6 all-gather.12
  425.6 36.3 reduce-scatter.14
  464.1 34.5 reduce-scatter.16
  500.3 46.7 all-gather.14
  548.8 27.2 all-gather.16
  585.9 30.9 reduce-scatter.18
  621.2 30.6 reduce-scatter.20
  653.5 22.0 all-gather.18
  680.3 22.8 all-gather.20
  714.5 34.9 reduce-scatter.22
  751.6 34.8 reduce-scatter.24
  787.9 27.4 all-gather.22
  816.8 28.5 all-gather.24
  848.6 49.3 reduce-scatter.26
  900.1 48.4 reduce-scatter.28
  950.2 45.3 all-gather.26
  997.0 65.3 all-gather.28

commit v3 on v2

--- a/solution.py
+++ b/solution.py
@@ -121,14 +121,27 @@
         offset = offset + block_rows
         first_front = first_front + (1 << LEVELS - 1 - level_at)
 
+    def in_group(value, share):
+        count = lax.axis_size("front")
+        groups = [list(range(i, i + share)) for i in range(0, count, share)]
+        return lax.all_to_all(
+            value, "front", split_axis=0, concat_axis=0, tiled=True, axis_index_groups=groups
+        )
+
     given = []
     for level_at in range(LEVELS):
         bit_count, block_rows, offset, start, own_live, inner_live = facts[level_at]
         piece = load_rows[offset : offset + block_rows]
-        if block_rows < FS:
-            spread = jnp.zeros((FS, piece.shape[1]), bf16)
-            piece = lax.dynamic_update_slice_in_dim(spread, piece, start, 0)
-        given.append(lax.all_to_all(piece, "elem", split_axis=0, concat_axis=1, tiled=True))
+        share = 1 << bit_count
+        if share > 1:
+            piece = piece.reshape(elem_count // share, share, inner // share, -1)
+            piece = in_group(piece.swapaxes(0, 1), share).reshape(elem_count * (inner // share), -1)
+        turned = lax.all_to_all(piece, "elem", split_axis=0, concat_axis=1, tiled=True)
+        if share > 1:
+            at = (device & share - 1) * (inner // share)
+            zeros = jnp.zeros((inner, turned.shape[1]), bf16)
+            turned = lax.dynamic_update_slice_in_dim(zeros, turned, at, 0)
+        given.append(turned)
 
     width = given[0].shape[1] // CHUNKS
 
@@ -202,8 +215,15 @@
 
         def piece_of(parts, facts_at):
             whole = jnp.concatenate(parts, 1)
+            share = 1 << facts_at[2]
+            if share > 1:
+                at = (device & share - 1) * (inner // share)
+                whole = lax.dynamic_slice_in_dim(whole, at, inner // share, 0)
             turned = lax.all_to_all(whole, "elem", split_axis=1, concat_axis=0, tiled=True)
-            return lax.dynamic_slice_in_dim(turned, facts_at[3], facts_at[4], 0)
+            if share > 1:
+                turned = turned.reshape(share, elem_count // share, inner // share, -1)
+                turned = in_group(turned, share).swapaxes(0, 1).reshape(facts_at[4], -1)
+            return turned
 
         upper = (factor_rows, inner_live, bit_count, start, block_rows)
     answers = [answer_of(c, upper, wide) for c in chunks]

time: 1140 us -> 1120 us (0.982)
  blocking collectives: 133 us -> 116 us
    all_to_all x2 -> x3, waiting for transfers between devices: 25.1 us -> 71.5 us  [body(): lax.all_to_all(piece, 'elem', split_axis=0, concat_axis=1, tiled=True)]
    all_to_all x3 -> x2, waiting for transfers between devices: 78.1 us -> 35.9 us  [piece_of(): lax.all_to_all(whole, 'elem', split_axis=1, concat_axis=0, tiled=True)]
    all_to_all x1 -> x3, blocking collectives: 53.1 us -> 36.8 us  [the longest x2 21.4 us: in_group(): lax.all_to_all(value, 'front', split_axis=0, concat_axis=0, tiled=True, a...]
    all_gather x10, waiting for transfers between devices: 182 us -> 167 us  [widen(): return lax.all_gather(value, 'elem', axis=0, tiled=True)]
  transfers between devices with their start and end apart: 38 -> 40, of which waited for: 29 -> 31; matrix products, arithmetic and copies ran while one was open for 16% -> 16% of each run, Pallas kernels for 0% -> 0%
where the time goes in v3:
time: 1120 us; the launch traced here: 1110 us
  waiting for transfers between devices  678 us (61%)
  matrix products  161 us (14%)
  blocking collectives  116 us (10%)
  starting transfers between devices  47.4 us (4%)
  local copies, waits for them, and re-layouts  31.7 us (3%)
  other arithmetic  31.2 us (3%)
  Pallas kernels  29.5 us (3%)
  between operations  14.7 us (1%)
    reduce_scatter x10, waiting for transfers between devices, scatter_sum(): lax.psum_scatter(partial_value, 'elem', scatter_dimension=0, tiled=True)  255 us
    all_gather x10, waiting for transfers between devices, widen(): return lax.all_gather(value, 'elem', axis=0, tiled=True)  167 us
    ppermute x12, waiting for transfers between devices, swapped(): lax.ppermute(array, axis, [(i, i ^ 1 << bit) for i in range(lax.axis_size...  143 us
    all_gather x1, blocking collectives, body(): places = lax.all_gather(dof_rows, 'elem', axis=1, tiled=True)  79.5 us
    all_to_all x3, waiting for transfers between devices, body(): lax.all_to_all(piece, 'elem', split_axis=0, concat_axis=1, tiled=True)  71.5 us
    dot_general x6, matrix products, answer_of(): lax.dot_general(rows, wide_rows[chunk], (((0,), (0,)), ((), ())), preferr...  43.5 us
    dot_general x6, matrix products, body(): product = jnp.dot(factor_rows, rhs, preferred_element_type=f32).astype(bf16)  42.7 us
    dot_general x4, matrix products, body(): lax.dot_general(links, answers[c], (((0,), (0,)), ((), ())), preferred_el...  39.1 us
  transfers between devices with their start and end apart: 40, of which 31 were waited for; matrix products, arithmetic and copies ran while one was open for 16% of the time, Pallas kernels for 0%

profile of v3, /device:TPU:0, one launch (start us, length us, event | category | flops | bytes accessed | tf_op | source)
XLA Modules:
  0.0 1109.5 jit_solution(9959227852365281967)
XLA Ops:
  27.3 79.5 %all_gather.33 = s32[24,1024]{0,1:T(8,128)S(1)} all-gather(s32[24,128]{0,1:T(8,128)S(1)} %copy.44), channel_id=1, replica_groups=mesh['elem'=8,'front'=4] {'elem'}, dimensions={1}, use_global_device_ids=true | all-gather | bytes 110592 | tf_op jit(solution)/shard_map/all_gather | solution.py:102
  117.9 29.5 %shard_map.91 = f32[112,128,64]{2,1,0:T(8,128)S(1)} custom-call(s32[1024]{0:T(1024)S(1)} %get-tuple-element.82.blocks_ref, s32[1024,24]{1,0:T(8,128)S(1)} %compare_select_fusion.rows_ref, bf16[1024,24,64]{2,1,0:T(8,128)(2,1)S(1)} %bitcast.115), custom_call_target="tpu_custom_call" | custom-call | tf_op jit(solution)/shard_map/pallas_call | solution.py:62
  157.3 25.3 %all-to-all-done.1 = bf16[8,1024,64]{1,2,0:T(8,128)(2,1)S(1)} async-done(((bf16[8,1024,64]{1,2,0:T(8,128)(2,1)}), bf16[8,1024,64]{1,2,0:T(8,128)(2,1)S(1)}, u32[]{:S(2)}, u32[]{:S(2)}) %all-to-all-start.1) | async-done | bytes 1048608 | tf_op jit(solution)/shard_map/all_to_all | solution.py:139
  202.0 39.1 %reduce-scatter.11.cloned.1.call-done = bf16[1024,256]{0,1:T(8,128)(2,1)} async-done(((bf16[8192,256]{0,1:T(8,128)(2,1)}), bf16[1024,256]{0,1:T(8,128)(2,1)}) %reduce-scatter.11.cloned.1.call-update) | async-done | bytes 524304 | tf_op jit(solution)/shard_map/reduce_scatter | solution.py:153
  243.1 48.7 %reduce-scatter.13.cloned.1.call-done = bf16[1024,256]{0,1:T(8,128)(2,1)} async-done(((bf16[8192,256]{0,1:T(8,128)(2,1)}), bf16[1024,256]{0,1:T(8,128)(2,1)}) %reduce-scatter.13.cloned.1.call-update) | async-done | bytes 524304 | tf_op jit(solution)/shard_map/reduce_scatter | solution.py:153
  293.8 45.0 %all-gather.11.cloned.1.call-done = bf16[8192,256]{0,1:T(8,128)(2,1)} async-done(((bf16[1024,256]{0,1:T(8,128)(2,1)}), bf16[8192,256]{0,1:T(8,128)(2,1)}) %all-gather.11.cloned.1.call-update) | async-done | bytes 4194320 | tf_op jit(solution)/shard_map/all_gather | solution.py:156
  354.7 29.6 %all-to-all-done.3 = bf16[8,512,64]{1,2,0:T(8,128)(2,1)S(1)} async-done(((bf16[8,512,64]{1,2,0:T(8,128)(2,1)}), bf16[8,512,64]{1,2,0:T(8,128)(2,1)S(1)}, u32[]{:S(2)}, u32[]{:S(2)}) %all-to-all-start.3) | async-done | bytes 524320 | tf_op jit(solution)/shard_map/all_to_all | solution.py:139
  394.8 12.9 %collective-permute-done = bf16[1024,256]{0,1:T(8,128)(2,1)S(1)} collective-permute-done((bf16[1024,256]{0,1:T(8,128)(2,1)S(1)}, bf16[1024,256]{0,1:T(8,128)(2,1)S(1)}, u32[]{:S(2)}, u32[]{:S(2)}) %collective-permute-start) | collective-permute-done | bytes 524320 | tf_op jit(solution)/shard_map/ppermute | solution.py:16
  451.8 34.4 %reduce-scatter.17.cloned.1.call-done = bf16[512,256]{0,1:T(8,128)(2,1)} async-done(((bf16[4096,256]{0,1:T(8,128)(2,1)}), bf16[512,256]{0,1:T(8,128)(2,1)}) %reduce-scatter.17.cloned.1.call-update) | async-done | bytes 262160 | tf_op jit(solution)/shard_map/reduce_scatter | solution.py:153
  487.9 27.7 %all-gather.15.cloned.1.call-done = bf16[4096,256]{0,1:T(8,128)(2,1)} async-done(((bf16[512,256]{0,1:T(8,128)(2,1)}), bf16[4096,256]{0,1:T(8,128)(2,1)}) %all-gather.15.cloned.1.call-update) | async-done | bytes 2097168 | tf_op jit(solution)/shard_map/all_gather | solution.py:156
  529.4 16.7 %all-to-all-done.5 = bf16[8,256,64]{1,2,0:T(8,128)(2,1)S(1)} async-done(((bf16[8,256,64]{1,2,0:T(8,128)(2,1)}), bf16[8,256,64]{1,2,0:T(8,128)(2,1)S(1)}, u32[]{:S(2)}, u32[]{:S(2)}) %all-to-all-start.5) | async-done | bytes 262176 | tf_op jit(solution)/shard_map/all_to_all | solution.py:139
  553.6 12.8 %collective-permute-done.2 = bf16[1024,256]{0,1:T(8,128)(2,1)S(1)} collective-permute-done((bf16[1024,256]{0,1:T(8,128)(2,1)S(1)}, bf16[1024,256]{0,1:T(8,128)(2,1)S(1)}, u32[]{:S(2)}, u32[]{:S(2)}) %collective-permute-start.2) | collective-permute-done | bytes 524320 | tf_op jit(solution)/shard_map/ppermute | solution.py:16
  620.7 29.1 %reduce-scatter.21.cloned.1.call-done = bf16[256,256]{0,1:T(8,128)(2,1)} async-done(((bf16[2048,256]{0,1:T(8,128)(2,1)}), bf16[256,256]{0,1:T(8,128)(2,1)}) %reduce-scatter.21.cloned.1.call-update) | async-done | bytes 131088 | tf_op jit(solution)/shard_map/reduce_scatter | solution.py:153
  651.5 22.0 %all-gather.19.cloned.1.call-done = bf16[2048,256]{0,1:T(8,128)(2,1)} async-done(((bf16[256,256]{0,1:T(8,128)(2,1)}), bf16[2048,256]{0,1:T(8,128)(2,1)}) %all-gather.19.cloned.1.call-update) | async-done | bytes 1048592 | tf_op jit(solution)/shard_map/all_gather | solution.py:156
  678.1 13.3 %collective-permute-done.6 = bf16[1024,256]{0,1:T(8,128)(2,1)S(1)} collective-permute-done((bf16[1024,256]{0,1:T(8,128)(2,1)S(1)}, bf16[1024,256]{0,1:T(8,128)(2,1)S(1)}, u32[]{:S(2)}, u32[]{:S(2)}) %collective-permute-start.6) | collective-permute-done | bytes 524320 | tf_op jit(solution)/shard_map/ppermute | solution.py:16
  692.3 12.6 %collective-permute-done.7 = bf16[1024,256]{0,1:T(8,128)(2,1)S(1)} collective-permute-done((bf16[1024,256]{0,1:T(8,128)(2,1)S(1)}, bf16[1024,256]{0,1:T(8,128)(2,1)S(1)}, u32[]{:S(2)}, u32[]{:S(2)}) %collective-permute-start.7) | collective-permute-done | bytes 524320 | tf_op jit(solution)/shard_map/ppermute | solution.py:16
  749.8 34.2 %reduce-scatter.25.cloned.1.call-done = bf16[512,256]{0,1:T(8,128)(2,1)} async-done(((bf16[4096,256]{0,1:T(8,128)(2,1)}), bf16[512,256]{0,1:T(8,128)(2,1)}) %reduce-scatter.25.cloned.1.call-update) | async-done | bytes 262160 | tf_op jit(solution)/shard_map/reduce_scatter | solution.py:153
  785.9 27.2 %all-gather.23.cloned.1.call-done = bf16[4096,256]{0,1:T(8,128)(2,1)} async-done(((bf16[512,256]{0,1:T(8,128)(2,1)}), bf16[4096,256]{0,1:T(8,128)(2,1)}) %all-gather.23.cloned.1.call-update) | async-done | bytes 2097168 | tf_op jit(solution)/shard_map/all_gather | solution.py:156
  878.9 16.8 %reduce-scatter.27.cloned.1.call-done = bf16[1024,256]{0,1:T(8,128)(2,1)} async-done(((bf16[8192,256]{0,1:T(8,128)(2,1)}), bf16[1024,256]{0,1:T(8,128)(2,1)}) %reduce-scatter.27.cloned.1.call-update) | async-done | bytes 524304 | tf_op jit(solution)/shard_map/reduce_scatter | solution.py:153
  897.9 48.5 %reduce-scatter.29.cloned.1.call-done = bf16[1024,256]{0,1:T(8,128)(2,1)} async-done(((bf16[8192,256]{0,1:T(8,128)(2,1)}), bf16[1024,256]{0,1:T(8,128)(2,1)}) %reduce-scatter.29.cloned.1.call-update) | async-done | bytes 524304 | tf_op jit(solution)/shard_map/reduce_scatter | solution.py:153
  948.5 44.8 %all-gather.27.cloned.1.call-done = bf16[8192,256]{0,1:T(8,128)(2,1)} async-done(((bf16[1024,256]{0,1:T(8,128)(2,1)}), bf16[8192,256]{0,1:T(8,128)(2,1)}) %all-gather.27.cloned.1.call-update) | async-done | bytes 4194320 | tf_op jit(solution)/shard_map/all_gather | solution.py:156
  993.4 15.3 %all_to_all.148 = bf16[256,8,64]{0,2,1:T(8,128)(2,1)} all-to-all(bf16[256,8,64]{0,2,1:T(8,128)(2,1)S(1)} %bitcast.123), channel_id=1, replica_groups=mesh['elem'=8,'front'=4] {'elem'}, dimensions={1} | all-to-all | bytes 524288 | tf_op jit(solution)/shard_map/all_to_all | solution.py:222
  1033.7 16.0 %all-to-all-done.7 = bf16[512,8,64]{0,2,1:T(8,128)(2,1)} async-done(((bf16[512,8,64]{0,2,1:T(8,128)(2,1)}), bf16[512,8,64]{0,2,1:T(8,128)(2,1)}, u32[]{:S(2)}, u32[]{:S(2)}) %all-to-all-start.7) | async-done | bytes 524320 | tf_op jit(solution)/shard_map/all_to_all | solution.py:222
  1077.9 19.9 %all-to-all-done.6 = bf16[1024,8,64]{0,2,1:T(8,128)(2,1)} async-done(((bf16[1024,8,64]{0,2,1:T(8,128)(2,1)}), bf16[1024,8,64]{0,2,1:T(8,128)(2,1)}, u32[]{:S(2)}, u32[]{:S(2)}) %all-to-all-start.6) | async-done | bytes 1048608 | tf_op jit(solution)/shard_map/all_to_all | solution.py:222
  (180 shorter events, 394.1 us)
Async XLA Ops:
  20.8 86.4 %all-to-all-start = ((bf16[128,24,512]{0,1,2:T(8,128)(2,1)}), bf16[128,24,512]{0,1,2:T(8,128)(2,1)}, u32[]{:S(2)}, u32[]{:S(2)}) async-start(bf16[128,24,512]{0,1,2:T(8,128)(2,1)} %copy.46), calls=%async_computation | async-start | bytes 6291456 | tf_op jit(solution)/shard_map/all_to_all | solution.py:103
  156.0 85.1 %reduce-scatter.11.cloned.1.call-start = ((), (), s32[]{:S(2)}) async-start(), calls=%async_computation.21 | async-start | bytes 4718592 | tf_op jit(solution)/shard_map/reduce_scatter | solution.py:153
  192.1 99.7 %reduce-scatter.13.cloned.1.call-start = ((), (), s32[]{:S(2)}) async-start(), calls=%async_computation.22 | async-start | bytes 4718592 | tf_op jit(solution)/shard_map/reduce_scatter | solution.py:153
  241.1 97.7 %all-gather.11.cloned.1.call-start = ((), (), s32[]{:S(2)}) async-start(), calls=%async_computation.23 | async-start | bytes 4718592 | tf_op jit(solution)/shard_map/all_gather | solution.py:156
  291.8 123.0 %all-gather.13.cloned.1.call-start = ((), (), s32[]{:S(2)}) async-start(), calls=%async_computation.24 | async-start | bytes 4718592 | tf_op jit(solution)/shard_map/all_gather | solution.py:156
  351.0 33.4 %all-to-all-start.3 = ((bf16[8,512,64]{1,2,0:T(8,128)(2,1)}), bf16[8,512,64]{1,2,0:T(8,128)(2,1)S(1)}, u32[]{:S(2)}, u32[]{:S(2)}) async-start(bf16[8,512,64]{1,2,0:T(8,128)(2,1)} %bitcast.17), calls=%async_computation.5 | async-start | bytes 1048576 | tf_op jit(solution)/shard_map/all_to_all | solution.py:139
  354.5 94.9 %reduce-scatter.15.cloned.1.call-start = ((), (), s32[]{:S(2)}) async-start(), calls=%async_computation.25 | async-start | bytes 2359296 | tf_op jit(solution)/shard_map/reduce_scatter | solution.py:153
  414.8 71.3 %reduce-scatter.17.cloned.1.call-start = ((), (), s32[]{:S(2)}) async-start(), calls=%async_computation.26 | async-start | bytes 2359296 | tf_op jit(solution)/shard_map/reduce_scatter | solution.py:153
  449.4 66.2 %all-gather.15.cloned.1.call-start = ((), (), s32[]{:S(2)}) async-start(), calls=%async_computation.27 | async-start | bytes 2359296 | tf_op jit(solution)/shard_map/all_gather | solution.py:156
  486.2 97.8 %all-gather.17.cloned.1.call-start = ((), (), s32[]{:S(2)}) async-start(), calls=%async_computation.28 | async-start | bytes 2359296 | tf_op jit(solution)/shard_map/all_gather | solution.py:156
  528.9 89.5 %reduce-scatter.19.cloned.1.call-start = ((), (), s32[]{:S(2)}) async-start(), calls=%async_computation.29 | async-start | bytes 1179648 | tf_op jit(solution)/shard_map/reduce_scatter | solution.py:153
  584.0 65.8 %reduce-scatter.21.cloned.1.call-start = ((), (), s32[]{:S(2)}) async-start(), calls=%async_computation.30 | async-start | bytes 1179648 | tf_op jit(solution)/shard_map/reduce_scatter | solution.py:153
  618.5 55.0 %all-gather.19.cloned.1.call-start = ((), (), s32[]{:S(2)}) async-start(), calls=%async_computation.31 | async-start | bytes 1179648 | tf_op jit(solution)/shard_map/all_gather | solution.py:156
  649.8 62.4 %all-gather.21.cloned.1.call-start = ((), (), s32[]{:S(2)}) async-start(), calls=%async_computation.32 | async-start | bytes 1179648 | tf_op jit(solution)/shard_map/all_gather | solution.py:156
  678.1 69.9 %reduce-scatter.23.cloned.1.call-start = ((), (), s32[]{:S(2)}) async-start(), calls=%async_computation.33 | async-start | bytes 2359296 | tf_op jit(solution)/shard_map/reduce_scatter | solution.py:153
  712.2 71.8 %reduce-scatter.25.cloned.1.call-start = ((), (), s32[]{:S(2)}) async-start(), calls=%async_computation.34 | async-start | bytes 2359296 | tf_op jit(solution)/shard_map/reduce_scatter | solution.py:153
  748.0 65.1 %all-gather.23.cloned.1.call-start = ((), (), s32[]{:S(2)}) async-start(), calls=%async_computation.35 | async-start | bytes 2359296 | tf_op jit(solution)/shard_map/all_gather | solution.py:156
  784.0 62.2 %all-gather.25.cloned.1.call-start = ((), (), s32[]{:S(2)}) async-start(), calls=%async_computation.36 | async-start | bytes 2359296 | tf_op jit(solution)/shard_map/all_gather | solution.py:156
  813.1 82.6 %reduce-scatter.27.cloned.1.call-start = ((), (), s32[]{:S(2)}) async-start(), calls=%async_computation.37 | async-start | bytes 4718592 | tf_op jit(solution)/shard_map/reduce_scatter | solution.py:153
  846.3 100.1 %reduce-scatter.29.cloned.1.call-start = ((), (), s32[]{:S(2)}) async-start(), calls=%async_computation.38 | async-start | bytes 4718592 | tf_op jit(solution)/shard_map/reduce_scatter | solution.py:153
  895.8 97.5 %all-gather.27.cloned.1.call-start = ((), (), s32[]{:S(2)}) async-start(), calls=%async_computation.39 | async-start | bytes 4718592 | tf_op jit(solution)/shard_map/all_gather | solution.py:156
  946.4 107.8 %all-gather.29.cloned.1.call-start = ((), (), s32[]{:S(2)}) async-start(), calls=%async_computation.40 | async-start | bytes 4718592 | tf_op jit(solution)/shard_map/all_gather | solution.py:156
  1017.7 32.0 %all-to-all-start.7 = ((bf16[512,8,64]{0,2,1:T(8,128)(2,1)}), bf16[512,8,64]{0,2,1:T(8,128)(2,1)}, u32[]{:S(2)}, u32[]{:S(2)}) async-start(bf16[512,8,64]{0,2,1:T(8,128)(2,1)} %bitcast.46), calls=%async_computation.17 | async-start | bytes 1048576 | tf_op jit(solution)/shard_map/all_to_all | solution.py:222
  1066.7 31.1 %all-to-all-start.6 = ((bf16[1024,8,64]{0,2,1:T(8,128)(2,1)}), bf16[1024,8,64]{0,2,1:T(8,128)(2,1)}, u32[]{:S(2)}, u32[]{:S(2)}) async-start(bf16[1024,8,64]{0,2,1:T(8,128)(2,1)} %bitcast.119), calls=%async_computation.16 | async-start | bytes 2097152 | tf_op jit(solution)/shard_map/all_to_all | solution.py:222
  (28 other events, 658.3 us)
Sparse Core Ops, SparseCore 0:
  192.2 48.8 reduce-scatter.10
  243.4 48.3 reduce-scatter.12
  293.4 45.3 all-gather.10
  340.3 56.8 all-gather.12
  415.0 34.3 reduce-scatter.14
  451.5 34.5 reduce-scatter.16
  487.8 27.7 all-gather.14
  517.2 34.5 all-gather.16
  584.1 30.5 reduce-scatter.18
  618.6 31.1 reduce-scatter.20
  651.4 22.0 all-gather.18
  678.2 22.9 all-gather.20
  712.4 34.9 reduce-scatter.22
  749.5 34.5 reduce-scatter.24
  785.5 27.5 all-gather.22
  814.5 28.5 all-gather.24
  846.4 49.3 reduce-scatter.26
  897.9 48.4 reduce-scatter.28
  947.9 45.3 all-gather.26
  994.8 57.7 all-gather.28
